TPU v7x, 512 devices: a whole 4x4x16 slice. The times are simulated.
512 devices in a mesh: row: 16 (over y, x), col: 16 (over z), depth: 2 (over core).
Axes of the slice: x: 4, y: 4, z: 16, core: 2. Of those that a mesh axis runs over, the one named last changes fastest.
Arguments:
- left_store: float32 [16, 2, 16, 2, 64, 1024], P('row', 'depth', 'col'), may hold values from -6 to 6
- left_home: int32 [16, 2, 16], P('row', 'depth'), may hold values from 0 to 15, each once within a row
- up_store: float32 [16, 2, 16, 2, 64, 1024], P('col', 'depth', 'row'), may hold values from -0.3125 to 0.3125
- up_home: int32 [16, 2, 16], P('col', 'depth'), may hold values from 0 to 15, each once within a row
- targets: int32 [16, 16, 2], P('row', 'col'), may hold values from 0 to 63, as said below
- sketch: float32 [16, 16, 2, 64, 1024], P('row', 'col'), may hold values from -0.1875 to 0.1875
Outputs:
- basis: float32 [16, 16, 2, 64, 1024], P('row', 'col', 'depth')
- weights: float32 [16, 16, 2, 64, 1024], P('row', 'col', 'depth')
Inputs may be any that keep to these rules, and one draw needn't show every extreme that they name: `left_home`: for each row and depth index the entries are the store positions 0 to 15, each once. `up_home`: for each col and depth index the entries are the store positions 0 to 15, each once. `targets`: the 2 entries of one row and col index are distinct.
All inputs are finite; a program needn't handle non-finite values.
Results may differ from a plain program's by a relative error of at most 0.0003.
Values sent between devices are 32-bit elements; how exact they have to be, the bound alone decides.
No kernel may reach another device: no remote copies, remote signals or barrier semaphores. Data moves between devices by JAX's collectives and lax.ppermute only.
A program may use at most 128 MiB of HBM per device.

v0:
```python
import math

import jax
import jax.numpy as jnp
from jax import lax
from jax.experimental import pallas as pl
from jax.experimental.pallas import tpu as pltpu
from jax.sharding import PartitionSpec as P


KD = 2
CB = 8
SIDE = 4
UP_AT, TARGET_AT, ROW_AT, COL_AT, DEPTH_AT = 16, 32, 34, 35, 36


def z_shift(n_col, crossing=0):
    return [(c * 2 + (d ^ crossing), ((c + (1 - 2 * d)) % n_col) * 2 + d) for c in range(n_col) for d in (0, 1)]


def xy_shift(step, phase):
    pairs = []
    for r in range(SIDE * SIDE):
        y, x = divmod(r, SIDE)
        for d in (0, 1):
            if (d + phase) % 2 == 0:
                to = y * SIDE + (x + step) % SIDE
            else:
                to = (y + step) % SIDE * SIDE + x
            pairs.append((r * 2 + d, to * 2 + d))
    return pairs


SWAP = [(0, 1), (1, 0)]


def ring_steps(info, position):
    way = info[COL_AT] - position
    return jnp.where(info[DEPTH_AT] == 0, way, -way) & 15


def up_place(info, position):
    row = info[ROW_AT]
    dy = (row // SIDE - position // SIDE) & (SIDE - 1)
    dx = (row - position) & (SIDE - 1)
    first = info[DEPTH_AT] == 0
    return jnp.where(first, dy, dx), jnp.where(first, dx, dy)


def draw(ws, ps, qs, drawn):
    n, size = ws.shape
    tested = dot(ws[...], qs[...].reshape(KD * n, size), (1, 1))
    for k in range(KD):
        drawn[k] = dot(tested[:, k * n : k * n + n], ps[k], (1, 0))


def up_kernel(info, u0, u1, u2, u3, out, ps, qs, sems, own_sems):
    ups = (u0, u1, u2, u3)
    depth = info[DEPTH_AT]
    j_own, j_other = info[TARGET_AT + depth] % CB, info[TARGET_AT + 1 - depth] % CB

    def copies(source, k):
        return (
            pltpu.make_async_copy(source.at[1], qs.at[k], own_sems.at[k, 1]),
            pltpu.make_async_copy(source.at[0], ps.at[k], own_sems.at[k, 0]),
        )

    for k in range(KD):
        t, s = up_place(info, info[UP_AT + j_other * KD + k])
        t_own, s_own = up_place(info, info[UP_AT + j_own * KD + k])
        for i in range(SIDE):

            @pl.when(t == i)
            def _():
                pltpu.make_async_copy(ups[i].at[s], out.at[k], sems.at[k]).start()

            @pl.when(t_own == i)
            def _():
                for copy in copies(ups[i].at[s_own], k):
                    copy.start()

    for k in range(KD):
        for copy in copies(u0.at[0], k):
            copy.wait()
    for k in range(KD):
        pltpu.make_async_copy(u0.at[0], out.at[k], sems.at[k]).wait()


def left_choice_kernel(info, other, *refs):
    own, across, out, sems = refs[:8], refs[8:15], refs[15], refs[16]
    tile = info[TARGET_AT + 1 - info[DEPTH_AT]]
    b = tile // CB
    for kind, (table, pieces) in enumerate(((info, own), (other, across))):
        for k in range(KD):
            slot = (1 - kind) * KD + k
            s = ring_steps(info, table[b * KD + k])
            for i, piece in enumerate(pieces):

                @pl.when(s == i + kind)
                def _():
                    pltpu.make_async_copy(piece, out.at[slot], sems.at[slot]).start()

    for kind, (table, pieces) in enumerate(((info, own), (other, across))):
        for k in range(KD):
            slot = (1 - kind) * KD + k
            s = ring_steps(info, table[b * KD + k])

            @pl.when((s >= kind) & (s <= 7))
            def _():
                pltpu.make_async_copy(pieces[0], out.at[slot], sems.at[slot]).wait()


def parts(x):
    high = x.astype(jnp.bfloat16)
    return high, (x - high.astype(jnp.float32)).astype(jnp.bfloat16)


def dot(a, b, contract):
    dims = ((contract[:1], contract[1:]), ((), ()))
    one = lambda u, v: lax.dot_general(u, v, dims, preferred_element_type=jnp.float32)
    (a_high, a_low), (b_high, b_low) = parts(a), parts(b)
    return one(a_high, b_high) + (one(a_high, b_low) + one(a_low, b_high))


def inverse_factor(gram):
    n = gram.shape[0]
    row_id = lax.broadcasted_iota(jnp.int32, (n, n), 0)
    lane_id = lax.broadcasted_iota(jnp.int32, (n, n), 1)
    eye = jnp.where(row_id == lane_id, jnp.float32(1), jnp.float32(0))
    work = jnp.concatenate([gram, eye], axis=1)
    tall, wide = 8, 2 * n
    blocks = [work[tall * i : tall * i + tall] for i in range(n // tall)]
    sub = lax.broadcasted_iota(jnp.int32, (tall, wide), 0)
    spread = lambda x: jnp.broadcast_to(x, (tall, wide))
    for at in range(n // tall):
        below = n // tall - at
        columns = [[spread(blocks[at + i][:, tall * at + j : tall * at + j + 1]) for i in range(below)] for j in range(tall)]
        block, rows, steps = blocks[at], [], []
        for w in range(0, tall, 2):
            first, second = columns[w], columns[w + 1]
            a, b, c = spread(first[0][w : w + 1]), spread(first[0][w + 1 : w + 2]), spread(second[0][w + 1 : w + 2])
            det_root = lax.rsqrt(a * c - b * b)
            scale = det_root * det_root
            ia, ib, ic = c * scale, -b * scale, a * scale
            for j in range(w + 2, tall):
                p, q = spread(columns[j][0][w : w + 1]), spread(columns[j][0][w + 1 : w + 2])
                s, t = ia * p + ib * q, ib * p + ic * q
                columns[j] = [columns[j][i] - first[i] * s - second[i] * t for i in range(below)]
            p, q = spread(block[w : w + 1]), spread(block[w + 1 : w + 2])
            s, t = ia * p + ib * q, ib * p + ic * q
            if w + 2 < tall:
                block = block - first[0] * s - second[0] * t
            steps.append((first, second, s, t))
            a_root = lax.rsqrt(a)
            rows += [p * a_root, (q - b * (a_root * a_root) * p) * (det_root * (a * a_root))]
        done = rows[-1]
        for w in range(tall - 1):
            done = jnp.where(sub == w, rows[w], done)
        blocks[at] = done
        for i in range(1, below):
            for first, second, s, t in steps:
                blocks[at + i] = blocks[at + i] - first[i] * s - second[i] * t
    return jnp.concatenate(blocks, axis=0)[:, n:]


def across_kernel(info, up_in, sketch, ps_own, qs_own, ps, qs, drawn_own, drawn, ws, sems, sketch_sem):
    sketch_copy = pltpu.make_async_copy(sketch.at[info[DEPTH_AT]], ws, sketch_sem)
    copies = [pltpu.make_async_copy(up_in.at[k, 1 - i], (qs, ps)[i].at[k], sems.at[k, i]) for k in range(KD) for i in range(2)]
    for copy in (sketch_copy, *copies):
        copy.start()
    sketch_copy.wait()
    draw(ws, ps_own, qs_own, drawn_own)
    for copy in copies:
        copy.wait()
    draw(ws, ps, qs, drawn)


def tile_kernel(info, other, *refs):
    own, across = refs[:9], refs[9:16]
    left_in, last_in = refs[16:18]
    ps, qs, drawn = refs[18:24:3], refs[19:24:3], refs[20:24:3]
    basis_out, weights_out, pairs, basis, weights, left_sems, out_sems = refs[24:]
    b = info[TARGET_AT + info[DEPTH_AT]] // CB
    slots, _, n, size = pairs.shape

    def start(condition, source, slot):
        @pl.when(condition)
        def _():
            pltpu.make_async_copy(source, pairs.at[slot], left_sems.at[slot]).start()

    for kind, (table, pieces) in enumerate(((info, own), (other, across))):
        for k in range(KD):
            slot = kind * KD + k
            s = ring_steps(info, table[b * KD + k])
            for i, piece in enumerate(pieces):
                start(s == i + kind, piece, slot)
            if kind == 1:
                start(s == 8, last_in, slot)
            start((s > 8) | (s < kind), left_in.at[slot], slot)
    for slot in range(slots):
        pltpu.make_async_copy(own[0], pairs.at[slot], left_sems.at[slot]).wait()
    folded = [dot(drawn[i // KD][i % KD], pairs[i, 1], (1, 1)) for i in range(slots)]
    x_all = jnp.concatenate([pairs[i, 0] for i in range(slots)], axis=0)
    sample = dot(jnp.concatenate(folded, axis=1), x_all, (1, 0))
    inverse = inverse_factor(dot(sample, sample, (1, 1)))
    middles = [dot(pairs[i, 1], ps[i // KD][i % KD], (1, 1)) for i in range(slots)]
    turned = [dot(dot(sample, pairs[i, 0], (1, 1)), middles[i], (1, 0)) for i in range(slots)]
    turned = [jnp.concatenate(turned[i : i + KD], axis=1) for i in (0, KD)]
    root = math.sqrt(size)
    basis[...] = dot(inverse * root, sample, (1, 0))
    done = [pltpu.make_async_copy(basis, basis_out, out_sems.at[0])]
    done[0].start()
    wide = size // 4
    for i in range(4):
        at = slice(i * wide, i * wide + wide)
        project = sum(dot(t, q[:, :, at].reshape(KD * n, wide), (1, 0)) for t, q in zip(turned, qs))
        weights[:, at] = dot(inverse * (1 / root), project, (1, 0))
        done.append(pltpu.make_async_copy(weights.at[:, at], weights_out.at[:, at], out_sems.at[i + 1]))
        done[-1].start()
    for copy in done:
        copy.wait()


def local_kernel(kernel, in_spaces, out_shape, out_spaces, scratch, mebibytes=1):
    return pl.pallas_call(
        kernel,
        out_shape=out_shape,
        in_specs=[pl.BlockSpec(memory_space=space) for space in in_spaces],
        out_specs=tuple(pl.BlockSpec(memory_space=space) for space in out_spaces),
        scratch_shapes=scratch,
        compiler_params=pltpu.CompilerParams(vmem_limit_bytes=mebibytes << 20),
    )


def pieces_and_tile(left_store, left_home, up_store, up_home, targets, sketch):
    n_col = lax.axis_size("col")
    own, up, test = left_store[0, 0, 0], up_store[0, 0, 0], sketch[0, 0]
    pair = own.shape
    places = jnp.stack([lax.axis_index(a).astype(jnp.int32) for a in ("row", "col", "depth")])
    info = jnp.concatenate([left_home[0, 0], up_home[0, 0], targets[0, 0], places])
    axes, shift, half = ("col", "depth"), z_shift(n_col), n_col // 2
    own_pieces, across_pieces = [own], [lax.ppermute(own, axes, z_shift(n_col, 1))]
    for step in range(1, half + 1):
        own_pieces.append(lax.ppermute(own_pieces[-1], axes, shift))
        if 1 < step < half:
            across_pieces.append(lax.ppermute(across_pieces[-1], axes, shift))
    block = jnp.stack([up] + [lax.ppermute(up, ("row", "depth"), xy_shift(s, 0)) for s in range(1, SIDE)])
    ups = [block] + [lax.ppermute(block, ("row", "depth"), xy_shift(s, 1)) for s in range(1, SIDE)]
    other = lax.ppermute(info, "depth", SWAP)

    early = lambda pieces, n: [pltpu.with_memory_space_constraint(x, pltpu.HBM) for x in pieces[:n]] + pieces[n:]
    own_held, across_held = early(own_pieces, 7), early(across_pieces, 6)
    f32 = jnp.float32
    smem, hbm, vmem = pltpu.SMEM, pltpu.HBM, pltpu.VMEM
    slots = 2 * KD
    dma = pltpu.SemaphoreType.DMA
    flat = pair[1:]
    array = lambda *shape: jax.ShapeDtypeStruct(shape, f32)
    tile, couple = array(*flat), array(KD, *flat)
    tile_scratch = vmem(flat, f32)

    outs = array(KD, *pair), couple, couple
    scratch = [dma((KD,)), dma((KD, 2))]
    up_part = local_kernel(up_kernel, [smem] + [hbm] * SIDE, outs, [hbm] + [vmem] * 2, scratch, 6)
    choice, p_own, q_own = up_part(info, *ups)
    up_in = lax.ppermute(choice, "depth", SWAP)
    left_choice = local_kernel(left_choice_kernel, [smem] * 2 + [hbm] * 15, (array(slots, *pair),), [hbm], [dma((slots,))])
    left_in = lax.ppermute(left_choice(info, other, *own_held[:8], *across_held)[0], "depth", SWAP)
    last_in = lax.ppermute(own_pieces[8], "depth", SWAP)

    scratch = [tile_scratch, dma((KD, 2)), dma]
    across_part = local_kernel(across_kernel, [smem] + [hbm] * 2 + [vmem] * 2, (couple,) * 4, [vmem] * 4, scratch, 6)
    p_across, q_across, drawn_own, drawn_across = across_part(info, up_in, test, p_own, q_own)
    sides = p_own, q_own, drawn_own, p_across, q_across, drawn_across
    scratch = [vmem((slots, *pair), f32)] + [tile_scratch] * 2 + [dma((slots,)), dma((5,))]
    whole = local_kernel(tile_kernel, [smem] * 2 + [hbm] * 18 + [vmem] * 6, (tile, tile), [hbm] * 2, scratch, 12)
    basis, weights = whole(info, other, *own_held, *across_held, left_in, last_in, *sides)
    return basis[None, None, None], weights[None, None, None]


def solution(mesh):
    return jax.shard_map(
        pieces_and_tile,
        mesh=mesh,
        in_specs=(
            P("row", "depth", "col", None, None, None),
            P("row", "depth", None),
            P("col", "depth", "row", None, None, None),
            P("col", "depth", None),
            P("row", "col", None),
            P("row", "col", None, None, None),
        ),
        out_specs=(P("row", "col", "depth", None, None), P("row", "col", "depth", None, None)),
        check_vma=False,
    )
```

profile of v0, /device:TPU:1, one launch (start us, length us, event | category | flops | bytes accessed | tf_op | source)
XLA Modules:
  0.0 160.3 jit_solution(11309948797513885298)
XLA Ops:
  0.6 11.9 %collective-permute-start.1 = (f32[2,64,1024]{2,1,0:T(8,128)}, f32[2,64,1024]{2,1,0:T(8,128)S(1)}, u32[]{:S(2)}, u32[]{:S(2)}) collective-permute-start(f32[2,64,1024]{2,1,0:T(8,128)} %bitcast.16), channel_id=1, source_target_pairs={{0,2},{1,31},{2,4},{3,1},{4,6},{5,3},{6,8},{7,5},{8,10},{9,7},{10,... | collective-permute-start | bytes 1572872 | tf_op jit(solution)/shard_map/ppermute | solution.py:244
  12.6 1.9 %collective-permute-start.9 = (f32[2,64,1024]{2,1,0:T(8,128)}, f32[2,64,1024]{2,1,0:T(8,128)S(1)}, u32[]{:S(2)}, u32[]{:S(2)}) collective-permute-start(f32[2,64,1024]{2,1,0:T(8,128)} %bitcast.17), channel_id=1, source_target_pairs={{1,2},{0,31},{3,4},{2,1},{5,6},{4,3},{7,8},{6,5},{9,10},{8,7},{11,... | collective-permute-start | bytes 1572872 | tf_op jit(solution)/shard_map/ppermute | solution.py:242
  14.5 6.9 %collective-permute-done.1.refs_1_ = f32[2,64,1024]{2,1,0:T(8,128)S(1)} collective-permute-done((f32[2,64,1024]{2,1,0:T(8,128)}, f32[2,64,1024]{2,1,0:T(8,128)S(1)}, u32[]{:S(2)}, u32[]{:S(2)}) %collective-permute-start.1) | collective-permute-done | bytes 524320 | tf_op jit(solution)/shard_map/ppermute | solution.py:244
  21.4 4.9 %collective-permute-start.2 = (f32[2,64,1024]{2,1,0:T(8,128)S(1)}, f32[2,64,1024]{2,1,0:T(8,128)S(1)}, u32[]{:S(2)}, u32[]{:S(2)}) collective-permute-start(f32[2,64,1024]{2,1,0:T(8,128)S(1)} %collective-permute-done.1.refs_1_), channel_id=1, source_target_pairs={{0,2},{1,31},{2,4},{3,1},{4,6},{5,3},{6,8},{7,5},{8,10},{9,7},{10,... | collective-permute-start | bytes 1572872 | tf_op jit(solution)/shard_map/ppermute | solution.py:244
  26.3 0.0 collective-permute-done.9.refs_8_.refs_9_
  26.3 0.0 copy-start.2
  26.3 3.2 %collective-permute-start.10 = (f32[2,64,1024]{2,1,0:T(8,128)S(1)}, f32[2,64,1024]{2,1,0:T(8,128)S(1)}, u32[]{:S(2)}, u32[]{:S(2)}) collective-permute-start(f32[2,64,1024]{2,1,0:T(8,128)S(1)} %collective-permute-done.9.refs_8_.refs_9_), channel_id=1, source_target_pairs={{0,2},{1,31},{2,4},{3,1},{4,6},{5,3},{6,8},{7,5},{8,10},{9,7},{10,... | collective-permute-start | bytes 1572872 | tf_op jit(solution)/shard_map/ppermute | solution.py:246
  29.5 2.9 %collective-permute-done.2.refs_2_ = f32[2,64,1024]{2,1,0:T(8,128)S(1)} collective-permute-done((f32[2,64,1024]{2,1,0:T(8,128)S(1)}, f32[2,64,1024]{2,1,0:T(8,128)S(1)}, u32[]{:S(2)}, u32[]{:S(2)}) %collective-permute-start.2) | collective-permute-done | bytes 524320 | tf_op jit(solution)/shard_map/ppermute | solution.py:244
  32.4 5.0 %collective-permute-start.3 = (f32[2,64,1024]{2,1,0:T(8,128)S(1)}, f32[2,64,1024]{2,1,0:T(8,128)S(1)}, u32[]{:S(2)}, u32[]{:S(2)}) collective-permute-start(f32[2,64,1024]{2,1,0:T(8,128)S(1)} %collective-permute-done.2.refs_2_), channel_id=1, source_target_pairs={{0,2},{1,31},{2,4},{3,1},{4,6},{5,3},{6,8},{7,5},{8,10},{9,7},{10,... | collective-permute-start | bytes 1572872 | tf_op jit(solution)/shard_map/ppermute | solution.py:244
  37.4 0.6 collective-permute-done.10.refs_9_.refs_10_
  38.0 5.0 %collective-permute-start.11 = (f32[2,64,1024]{2,1,0:T(8,128)S(1)}, f32[2,64,1024]{2,1,0:T(8,128)S(1)}, u32[]{:S(2)}, u32[]{:S(2)}) collective-permute-start(f32[2,64,1024]{2,1,0:T(8,128)S(1)} %collective-permute-done.10.refs_9_.refs_10_), channel_id=1, source_target_pairs={{0,2},{1,31},{2,4},{3,1},{4,6},{5,3},{6,8},{7,5},{8,10},{9,7},{10,... | collective-permute-start | bytes 1572872 | tf_op jit(solution)/shard_map/ppermute | solution.py:246
  43.1 0.6 collective-permute-done.3.refs_3_
  43.7 5.0 %collective-permute-start.4 = (f32[2,64,1024]{2,1,0:T(8,128)S(1)}, f32[2,64,1024]{2,1,0:T(8,128)}, u32[]{:S(2)}, u32[]{:S(2)}) collective-permute-start(f32[2,64,1024]{2,1,0:T(8,128)S(1)} %collective-permute-done.3.refs_3_), channel_id=1, source_target_pairs={{0,2},{1,31},{2,4},{3,1},{4,6},{5,3},{6,8},{7,5},{8,10},{9,7},{10,... | collective-permute-start | bytes 1572872 | tf_op jit(solution)/shard_map/ppermute | solution.py:244
  48.7 0.6 collective-permute-done.11.refs_10_.refs_11_
  49.3 5.0 %collective-permute-start.12 = (f32[2,64,1024]{2,1,0:T(8,128)S(1)}, f32[2,64,1024]{2,1,0:T(8,128)}, u32[]{:S(2)}, u32[]{:S(2)}) collective-permute-start(f32[2,64,1024]{2,1,0:T(8,128)S(1)} %collective-permute-done.11.refs_10_.refs_11_), channel_id=1, source_target_pairs={{0,2},{1,31},{2,4},{3,1},{4,6},{5,3},{6,8},{7,5},{8,10},{9,7},{10,... | collective-permute-start | bytes 1572872 | tf_op jit(solution)/shard_map/ppermute | solution.py:246
  54.3 4.8 %collective-permute-start.19 = (f32[2,64,1024]{2,1,0:T(8,128)}, f32[2,64,1024]{2,1,0:T(8,128)}, u32[]{:S(2)}, u32[]{:S(2)}) collective-permute-start(f32[2,64,1024]{2,1,0:T(8,128)} %bitcast.20), channel_id=1, source_target_pairs={{0,64},{1,257},{32,96},{33,289},{64,0},{65,321},{96,32},{97,353},{... | collective-permute-start | bytes 1572872 | tf_op jit(solution)/shard_map/ppermute | solution.py:247
  59.1 2.7 %collective-permute-start.20 = (f32[2,64,1024]{2,1,0:T(8,128)}, f32[2,64,1024]{2,1,0:T(8,128)}, u32[]{:S(2)}, u32[]{:S(2)}) collective-permute-start(f32[2,64,1024]{2,1,0:T(8,128)} %bitcast.21), channel_id=1, source_target_pairs={{0,96},{1,385},{32,0},{33,417},{64,32},{65,449},{96,64},{97,481},{... | collective-permute-start | bytes 1572872 | tf_op jit(solution)/shard_map/ppermute | solution.py:247
  61.8 2.6 %collective-permute-start.18 = (f32[2,64,1024]{2,1,0:T(8,128)}, f32[2,64,1024]{2,1,0:T(8,128)}, u32[]{:S(2)}, u32[]{:S(2)}) collective-permute-start(f32[2,64,1024]{2,1,0:T(8,128)} %bitcast.22), channel_id=1, source_target_pairs={{0,32},{1,129},{32,64},{33,161},{64,96},{65,193},{96,0},{97,225},{... | collective-permute-start | bytes 1572872 | tf_op jit(solution)/shard_map/ppermute | solution.py:247
  64.4 0.0 collective-permute-done.4.refs_4_
  64.4 1.9 %collective-permute-start.5 = (f32[2,64,1024]{2,1,0:T(8,128)}, f32[2,64,1024]{2,1,0:T(8,128)}, u32[]{:S(2)}, u32[]{:S(2)}) collective-permute-start(f32[2,64,1024]{2,1,0:T(8,128)} %collective-permute-done.4.refs_4_), channel_id=1, source_target_pairs={{0,2},{1,31},{2,4},{3,1},{4,6},{5,3},{6,8},{7,5},{8,10},{9,7},{10,... | collective-permute-start | bytes 1572872 | tf_op jit(solution)/shard_map/ppermute | solution.py:244
  66.4 0.0 collective-permute-done.12.refs_11_.refs_12_
  66.4 1.9 %collective-permute-start.13 = (f32[2,64,1024]{2,1,0:T(8,128)}, f32[2,64,1024]{2,1,0:T(8,128)}, u32[]{:S(2)}, u32[]{:S(2)}) collective-permute-start(f32[2,64,1024]{2,1,0:T(8,128)} %collective-permute-done.12.refs_11_.refs_12_), channel_id=1, source_target_pairs={{0,2},{1,31},{2,4},{3,1},{4,6},{5,3},{6,8},{7,5},{8,10},{9,7},{10,... | collective-permute-start | bytes 1572872 | tf_op jit(solution)/shard_map/ppermute | solution.py:246
  68.3 0.8 concatenate.3.info
  69.1 0.0 collective-permute-done.19
  69.1 5.1 %collective-permute-start = (s32[37]{0:T(128)S(1)}, s32[37]{0:T(128)S(1)}, u32[]{:S(2)}, u32[]{:S(2)}) collective-permute-start(s32[37]{0:T(128)S(1)} %concatenate.3.info), channel_id=1, source_target_pairs={{0,1},{1,0},{2,3},{3,2},{4,5},{5,4},{6,7},{7,6},{8,9},{9,8},{10,11... | collective-permute-start | bytes 452 | tf_op jit(solution)/shard_map/ppermute | solution.py:249
  74.2 0.0 collective-permute-done.20
  74.2 0.0 collective-permute-done.18
  74.2 1.7 %pad_maximum_fusion.u0 = f32[4,2,64,1024]{3,2,1,0:T(8,128)S(1)} fusion(f32[1,2,64,1024]{3,2,1,0:T(8,128)} %bitcast.11, f32[1,2,64,1024]{3,2,1,0:T(8,128)} %bitcast.10, f32[1,2,64,1024]{3,2,1,0:T(8,128)} %bitcast.9, f32[1,2,64,1024]{3,2,1,0:T(8,128)} %bitcast.23), kind=kLoop, calls=%fused_computation | loop fusion | flops 1572864 | bytes 4194304 | tf_op jit(solution)/shard_map/stack | solution.py:247
  75.9 0.0 copy-done.1
  75.9 0.0 copy-done.2
  75.9 0.0 copy-done.3
  75.9 0.0 copy-done.4
  75.9 0.0 copy-done.5
  75.9 0.0 copy-done.6
  75.9 2.5 %collective-permute-start.21 = (f32[4,2,64,1024]{3,2,1,0:T(8,128)S(1)}, f32[4,2,64,1024]{3,2,1,0:T(8,128)S(1)}, u32[]{:S(2)}, u32[]{:S(2)}) collective-permute-start(f32[4,2,64,1024]{3,2,1,0:T(8,128)S(1)} %pad_maximum_fusion.u0), channel_id=1, source_target_pairs={{0,128},{1,33},{32,160},{33,65},{64,192},{65,97},{96,224},{97,1},{... | collective-permute-start | bytes 6291464 | tf_op jit(solution)/shard_map/ppermute | solution.py:248
  78.4 4.6 %collective-permute-start.22 = (f32[4,2,64,1024]{3,2,1,0:T(8,128)S(1)}, f32[4,2,64,1024]{3,2,1,0:T(8,128)S(1)}, u32[]{:S(2)}, u32[]{:S(2)}) collective-permute-start(f32[4,2,64,1024]{3,2,1,0:T(8,128)S(1)} %pad_maximum_fusion.u0), channel_id=1, source_target_pairs={{0,256},{1,65},{32,288},{33,97},{64,320},{65,1},{96,352},{97,33},{... | collective-permute-start | bytes 6291464 | tf_op jit(solution)/shard_map/ppermute | solution.py:248
  83.0 0.0 collective-permute-done.other
  83.0 2.8 %collective-permute-start.23 = (f32[4,2,64,1024]{3,2,1,0:T(8,128)S(1)}, f32[4,2,64,1024]{3,2,1,0:T(8,128)S(1)}, u32[]{:S(2)}, u32[]{:S(2)}) collective-permute-start(f32[4,2,64,1024]{3,2,1,0:T(8,128)S(1)} %pad_maximum_fusion.u0), channel_id=1, source_target_pairs={{0,384},{1,97},{32,416},{33,1},{64,448},{65,33},{96,480},{97,65},{... | collective-permute-start | bytes 6291464 | tf_op jit(solution)/shard_map/ppermute | solution.py:248
  85.9 0.0 collective-permute-done.5.refs_5_
  85.9 3.9 %collective-permute-start.6 = (f32[2,64,1024]{2,1,0:T(8,128)}, f32[2,64,1024]{2,1,0:T(8,128)S(1)}, u32[]{:S(2)}, u32[]{:S(2)}) collective-permute-start(f32[2,64,1024]{2,1,0:T(8,128)} %collective-permute-done.5.refs_5_), channel_id=1, source_target_pairs={{0,2},{1,31},{2,4},{3,1},{4,6},{5,3},{6,8},{7,5},{8,10},{9,7},{10,... | collective-permute-start | bytes 1572872 | tf_op jit(solution)/shard_map/ppermute | solution.py:244
  89.8 0.0 collective-permute-done.13.refs_12_.refs_13_
  89.8 3.6 %collective-permute-start.14 = (f32[2,64,1024]{2,1,0:T(8,128)}, f32[2,64,1024]{2,1,0:T(8,128)S(1)}, u32[]{:S(2)}, u32[]{:S(2)}) collective-permute-start(f32[2,64,1024]{2,1,0:T(8,128)} %collective-permute-done.13.refs_12_.refs_13_), channel_id=1, source_target_pairs={{0,2},{1,31},{2,4},{3,1},{4,6},{5,3},{6,8},{7,5},{8,10},{9,7},{10,... | collective-permute-start | bytes 1572872 | tf_op jit(solution)/shard_map/ppermute | solution.py:246
  93.5 2.8 %collective-permute-done.6.refs_6_ = f32[2,64,1024]{2,1,0:T(8,128)S(1)} collective-permute-done((f32[2,64,1024]{2,1,0:T(8,128)}, f32[2,64,1024]{2,1,0:T(8,128)S(1)}, u32[]{:S(2)}, u32[]{:S(2)}) %collective-permute-start.6) | collective-permute-done | bytes 524320 | tf_op jit(solution)/shard_map/ppermute | solution.py:244
  96.3 5.1 %collective-permute-start.7 = (f32[2,64,1024]{2,1,0:T(8,128)S(1)}, f32[2,64,1024]{2,1,0:T(8,128)S(1)}, u32[]{:S(2)}, u32[]{:S(2)}) collective-permute-start(f32[2,64,1024]{2,1,0:T(8,128)S(1)} %collective-permute-done.6.refs_6_), channel_id=1, source_target_pairs={{0,2},{1,31},{2,4},{3,1},{4,6},{5,3},{6,8},{7,5},{8,10},{9,7},{10,... | collective-permute-start | bytes 1572872 | tf_op jit(solution)/shard_map/ppermute | solution.py:244
  101.4 0.5 collective-permute-done.14.refs_13_.refs_14_
  101.9 5.1 %collective-permute-start.15 = (f32[2,64,1024]{2,1,0:T(8,128)S(1)}, f32[2,64,1024]{2,1,0:T(8,128)S(1)}, u32[]{:S(2)}, u32[]{:S(2)}) collective-permute-start(f32[2,64,1024]{2,1,0:T(8,128)S(1)} %collective-permute-done.14.refs_13_.refs_14_), channel_id=1, source_target_pairs={{0,2},{1,31},{2,4},{3,1},{4,6},{5,3},{6,8},{7,5},{8,10},{9,7},{10,... | collective-permute-start | bytes 1572872 | tf_op jit(solution)/shard_map/ppermute | solution.py:246
  107.1 0.5 collective-permute-done.7.refs_7_
  107.5 5.6 %collective-permute-done.15.refs_14_.refs_15_ = f32[2,64,1024]{2,1,0:T(8,128)S(1)} collective-permute-done((f32[2,64,1024]{2,1,0:T(8,128)S(1)}, f32[2,64,1024]{2,1,0:T(8,128)S(1)}, u32[]{:S(2)}, u32[]{:S(2)}) %collective-permute-start.15) | collective-permute-done | bytes 524320 | tf_op jit(solution)/shard_map/ppermute | solution.py:246
  113.2 1.8 %shard_map.77 = f32[4,2,64,1024]{3,2,1,0:T(8,128)S(1)} custom-call(s32[37]{0:T(128)S(1)} %concatenate.3.info, s32[37]{0:T(128)S(1)} %collective-permute-done.other, f32[2,64,1024]{2,1,0:T(8,128)} %bitcast.18, f32[2,64,1024]{2,1,0:T(8,128)} %copy-done.1, f32[2,64,1024]{2,1,0:T(8,128)} %copy-done.3, f32[2,64,1024]{2,1,0:T(8,128)} %copy-done.5, ...), custom_call_target="tpu_custom_call" | custom-call | tf_op jit(solution)/shard_map/pallas_call | solution.py:268
  115.0 0.0 copy-start
  115.0 9.8 %collective-permute-start.16 = (f32[4,2,64,1024]{3,2,1,0:T(8,128)S(1)}, f32[4,2,64,1024]{3,2,1,0:T(8,128)S(1)}, u32[]{:S(2)}, u32[]{:S(2)}) collective-permute-start(f32[4,2,64,1024]{3,2,1,0:T(8,128)S(1)} %shard_map.77), channel_id=1, source_target_pairs={{0,1},{1,0},{2,3},{3,2},{4,5},{5,4},{6,7},{7,6},{8,9},{9,8},{10,11... | collective-permute-start | bytes 6291464 | tf_op jit(solution)/shard_map/ppermute | solution.py:268
  124.9 0.0 collective-permute-done.21.u1
  124.9 2.4 %collective-permute-done.22.u2 = f32[4,2,64,1024]{3,2,1,0:T(8,128)S(1)} collective-permute-done((f32[4,2,64,1024]{3,2,1,0:T(8,128)S(1)}, f32[4,2,64,1024]{3,2,1,0:T(8,128)S(1)}, u32[]{:S(2)}, u32[]{:S(2)}) %collective-permute-start.22) | collective-permute-done | bytes 2097184 | tf_op jit(solution)/shard_map/ppermute | solution.py:248
  127.2 2.0 %collective-permute-done.23.u3 = f32[4,2,64,1024]{3,2,1,0:T(8,128)S(1)} collective-permute-done((f32[4,2,64,1024]{3,2,1,0:T(8,128)S(1)}, f32[4,2,64,1024]{3,2,1,0:T(8,128)S(1)}, u32[]{:S(2)}, u32[]{:S(2)}) %collective-permute-start.23) | collective-permute-done | bytes 2097184 | tf_op jit(solution)/shard_map/ppermute | solution.py:248
  129.2 0.9 shard_map.78
  130.1 6.3 %collective-permute-start.24 = (f32[2,2,64,1024]{3,2,1,0:T(8,128)S(1)}, f32[2,2,64,1024]{3,2,1,0:T(8,128)S(1)}, u32[]{:S(2)}, u32[]{:S(2)}) collective-permute-start(f32[2,2,64,1024]{3,2,1,0:T(8,128)S(1)} %get-tuple-element.13), channel_id=1, source_target_pairs={{0,1},{1,0},{2,3},{3,2},{4,5},{5,4},{6,7},{7,6},{8,9},{9,8},{10,11... | collective-permute-start | bytes 3145736 | tf_op jit(solution)/shard_map/ppermute | solution.py:266
  136.3 4.9 %collective-permute-start.8 = (f32[2,64,1024]{2,1,0:T(8,128)S(1)}, f32[2,64,1024]{2,1,0:T(8,128)S(1)}, u32[]{:S(2)}, u32[]{:S(2)}) collective-permute-start(f32[2,64,1024]{2,1,0:T(8,128)S(1)} %collective-permute-done.7.refs_7_), channel_id=1, source_target_pairs={{0,2},{1,31},{2,4},{3,1},{4,6},{5,3},{6,8},{7,5},{8,10},{9,7},{10,... | collective-permute-start | bytes 1572872 | tf_op jit(solution)/shard_map/ppermute | solution.py:244
  141.2 6.1 %collective-permute-done.8.refs_8_ = f32[2,64,1024]{2,1,0:T(8,128)S(1)} collective-permute-done((f32[2,64,1024]{2,1,0:T(8,128)S(1)}, f32[2,64,1024]{2,1,0:T(8,128)S(1)}, u32[]{:S(2)}, u32[]{:S(2)}) %collective-permute-start.8) | collective-permute-done | bytes 524320 | tf_op jit(solution)/shard_map/ppermute | solution.py:244
  147.3 3.2 %collective-permute-start.17 = (f32[2,64,1024]{2,1,0:T(8,128)S(1)}, f32[2,64,1024]{2,1,0:T(8,128)S(1)}, u32[]{:S(2)}, u32[]{:S(2)}) collective-permute-start(f32[2,64,1024]{2,1,0:T(8,128)S(1)} %collective-permute-done.8.refs_8_), channel_id=1, source_target_pairs={{0,1},{1,0},{2,3},{3,2},{4,5},{5,4},{6,7},{7,6},{8,9},{9,8},{10,11... | collective-permute-start | bytes 1572872 | tf_op jit(solution)/shard_map/ppermute | solution.py:269
  150.6 0.0 collective-permute-done.24.up_in
  150.6 2.8 %shard_map.79 = (f32[2,64,1024]{2,1,0:T(8,128)S(1)}, f32[2,64,1024]{2,1,0:T(8,128)S(1)}, f32[2,64,1024]{2,1,0:T(8,128)S(1)}, f32[2,64,1024]{2,1,0:T(8,128)S(1)}) custom-call(s32[37]{0:T(128)S(1)} %concatenate.3.info, f32[2,2,64,1024]{3,2,1,0:T(8,128)S(1)} %collective-permute-done.24.up_in, f32[2,64,1024]{2,1,0:T(8,128)S(1)} %bitcast.15, ...), custom_call_target="tpu_custom_call" | custom-call | tf_op jit(solution)/shard_map/pallas_call | solution.py:273
  153.4 0.0 collective-permute-done.17.refs_17_
  153.4 0.0 collective-permute-done.16.refs_16_
  153.4 6.9 %shard_map.80 = (f32[64,1024]{1,0:T(8,128)}, f32[64,1024]{1,0:T(8,128)}) custom-call(s32[37]{0:T(128)S(1)} %concatenate.3.info, s32[37]{0:T(128)S(1)} %collective-permute-done.other, f32[2,64,1024]{2,1,0:T(8,128)} %bitcast.19, f32[2,64,1024]{2,1,0:T(8,128)} %copy-done.1, f32[2,64,1024]{2,1,0:T(8,128)} %copy-done.3, f32[2,64,1024]{2,1,0:T(8,128)} %copy-done.5, ...), custom_call_target="tpu_custom_call" | custom-call | tf_op jit(solution)/shard_map/pallas_call | solution.py:277
  (10 shorter events, 0.0 us)
Async XLA Ops:
  0.6 20.8 %collective-permute-start.1 = (f32[2,64,1024]{2,1,0:T(8,128)}, f32[2,64,1024]{2,1,0:T(8,128)S(1)}, u32[]{:S(2)}, u32[]{:S(2)}) collective-permute-start(f32[2,64,1024]{2,1,0:T(8,128)} %bitcast.16), channel_id=1, source_target_pairs={{0,2},{1,31},{2,4},{3,1},{4,6},{5,3},{6,8},{7,5},{8,10},{9,7},{10,... | collective-permute-start | bytes 1572872 | tf_op jit(solution)/shard_map/ppermute | solution.py:244
  12.6 13.7 %collective-permute-start.9 = (f32[2,64,1024]{2,1,0:T(8,128)}, f32[2,64,1024]{2,1,0:T(8,128)S(1)}, u32[]{:S(2)}, u32[]{:S(2)}) collective-permute-start(f32[2,64,1024]{2,1,0:T(8,128)} %bitcast.17), channel_id=1, source_target_pairs={{1,2},{0,31},{3,4},{2,1},{5,6},{4,3},{7,8},{6,5},{9,10},{8,7},{11,... | collective-permute-start | bytes 1572872 | tf_op jit(solution)/shard_map/ppermute | solution.py:242
  21.4 54.5 %copy-start.1 = (f32[2,64,1024]{2,1,0:T(8,128)}, f32[2,64,1024]{2,1,0:T(8,128)S(1)}, u32[]{:S(2)}) copy-start(f32[2,64,1024]{2,1,0:T(8,128)S(1)} %collective-permute-done.1.refs_1_) | copy-start | bytes 1572868
  21.4 11.0 %collective-permute-start.2 = (f32[2,64,1024]{2,1,0:T(8,128)S(1)}, f32[2,64,1024]{2,1,0:T(8,128)S(1)}, u32[]{:S(2)}, u32[]{:S(2)}) collective-permute-start(f32[2,64,1024]{2,1,0:T(8,128)S(1)} %collective-permute-done.1.refs_1_), channel_id=1, source_target_pairs={{0,2},{1,31},{2,4},{3,1},{4,6},{5,3},{6,8},{7,5},{8,10},{9,7},{10,... | collective-permute-start | bytes 1572872 | tf_op jit(solution)/shard_map/ppermute | solution.py:244
  26.3 49.5 %copy-start.2 = (f32[2,64,1024]{2,1,0:T(8,128)}, f32[2,64,1024]{2,1,0:T(8,128)S(1)}, u32[]{:S(2)}) copy-start(f32[2,64,1024]{2,1,0:T(8,128)S(1)} %collective-permute-done.9.refs_8_.refs_9_) | copy-start | bytes 1572868
  26.3 11.7 %collective-permute-start.10 = (f32[2,64,1024]{2,1,0:T(8,128)S(1)}, f32[2,64,1024]{2,1,0:T(8,128)S(1)}, u32[]{:S(2)}, u32[]{:S(2)}) collective-permute-start(f32[2,64,1024]{2,1,0:T(8,128)S(1)} %collective-permute-done.9.refs_8_.refs_9_), channel_id=1, source_target_pairs={{0,2},{1,31},{2,4},{3,1},{4,6},{5,3},{6,8},{7,5},{8,10},{9,7},{10,... | collective-permute-start | bytes 1572872 | tf_op jit(solution)/shard_map/ppermute | solution.py:246
  32.4 43.5 %copy-start.3 = (f32[2,64,1024]{2,1,0:T(8,128)}, f32[2,64,1024]{2,1,0:T(8,128)S(1)}, u32[]{:S(2)}) copy-start(f32[2,64,1024]{2,1,0:T(8,128)S(1)} %collective-permute-done.2.refs_2_) | copy-start | bytes 1572868
  32.4 11.2 %collective-permute-start.3 = (f32[2,64,1024]{2,1,0:T(8,128)S(1)}, f32[2,64,1024]{2,1,0:T(8,128)S(1)}, u32[]{:S(2)}, u32[]{:S(2)}) collective-permute-start(f32[2,64,1024]{2,1,0:T(8,128)S(1)} %collective-permute-done.2.refs_2_), channel_id=1, source_target_pairs={{0,2},{1,31},{2,4},{3,1},{4,6},{5,3},{6,8},{7,5},{8,10},{9,7},{10,... | collective-permute-start | bytes 1572872 | tf_op jit(solution)/shard_map/ppermute | solution.py:244
  38.0 37.9 %copy-start.4 = (f32[2,64,1024]{2,1,0:T(8,128)}, f32[2,64,1024]{2,1,0:T(8,128)S(1)}, u32[]{:S(2)}) copy-start(f32[2,64,1024]{2,1,0:T(8,128)S(1)} %collective-permute-done.10.refs_9_.refs_10_) | copy-start | bytes 1572868
  38.0 11.2 %collective-permute-start.11 = (f32[2,64,1024]{2,1,0:T(8,128)S(1)}, f32[2,64,1024]{2,1,0:T(8,128)S(1)}, u32[]{:S(2)}, u32[]{:S(2)}) collective-permute-start(f32[2,64,1024]{2,1,0:T(8,128)S(1)} %collective-permute-done.10.refs_9_.refs_10_), channel_id=1, source_target_pairs={{0,2},{1,31},{2,4},{3,1},{4,6},{5,3},{6,8},{7,5},{8,10},{9,7},{10,... | collective-permute-start | bytes 1572872 | tf_op jit(solution)/shard_map/ppermute | solution.py:246
  43.6 32.2 %copy-start.5 = (f32[2,64,1024]{2,1,0:T(8,128)}, f32[2,64,1024]{2,1,0:T(8,128)S(1)}, u32[]{:S(2)}) copy-start(f32[2,64,1024]{2,1,0:T(8,128)S(1)} %collective-permute-done.3.refs_3_) | copy-start | bytes 1572868
  43.7 20.8 %collective-permute-start.4 = (f32[2,64,1024]{2,1,0:T(8,128)S(1)}, f32[2,64,1024]{2,1,0:T(8,128)}, u32[]{:S(2)}, u32[]{:S(2)}) collective-permute-start(f32[2,64,1024]{2,1,0:T(8,128)S(1)} %collective-permute-done.3.refs_3_), channel_id=1, source_target_pairs={{0,2},{1,31},{2,4},{3,1},{4,6},{5,3},{6,8},{7,5},{8,10},{9,7},{10,... | collective-permute-start | bytes 1572872 | tf_op jit(solution)/shard_map/ppermute | solution.py:244
  49.3 26.6 %copy-start.6 = (f32[2,64,1024]{2,1,0:T(8,128)}, f32[2,64,1024]{2,1,0:T(8,128)S(1)}, u32[]{:S(2)}) copy-start(f32[2,64,1024]{2,1,0:T(8,128)S(1)} %collective-permute-done.11.refs_10_.refs_11_) | copy-start | bytes 1572868
  49.3 17.1 %collective-permute-start.12 = (f32[2,64,1024]{2,1,0:T(8,128)S(1)}, f32[2,64,1024]{2,1,0:T(8,128)}, u32[]{:S(2)}, u32[]{:S(2)}) collective-permute-start(f32[2,64,1024]{2,1,0:T(8,128)S(1)} %collective-permute-done.11.refs_10_.refs_11_), channel_id=1, source_target_pairs={{0,2},{1,31},{2,4},{3,1},{4,6},{5,3},{6,8},{7,5},{8,10},{9,7},{10,... | collective-permute-start | bytes 1572872 | tf_op jit(solution)/shard_map/ppermute | solution.py:246
  54.3 14.8 %collective-permute-start.19 = (f32[2,64,1024]{2,1,0:T(8,128)}, f32[2,64,1024]{2,1,0:T(8,128)}, u32[]{:S(2)}, u32[]{:S(2)}) collective-permute-start(f32[2,64,1024]{2,1,0:T(8,128)} %bitcast.20), channel_id=1, source_target_pairs={{0,64},{1,257},{32,96},{33,289},{64,0},{65,321},{96,32},{97,353},{... | collective-permute-start | bytes 1572872 | tf_op jit(solution)/shard_map/ppermute | solution.py:247
  59.1 15.1 %collective-permute-start.20 = (f32[2,64,1024]{2,1,0:T(8,128)}, f32[2,64,1024]{2,1,0:T(8,128)}, u32[]{:S(2)}, u32[]{:S(2)}) collective-permute-start(f32[2,64,1024]{2,1,0:T(8,128)} %bitcast.21), channel_id=1, source_target_pairs={{0,96},{1,385},{32,0},{33,417},{64,32},{65,449},{96,64},{97,481},{... | collective-permute-start | bytes 1572872 | tf_op jit(solution)/shard_map/ppermute | solution.py:247
  61.8 12.4 %collective-permute-start.18 = (f32[2,64,1024]{2,1,0:T(8,128)}, f32[2,64,1024]{2,1,0:T(8,128)}, u32[]{:S(2)}, u32[]{:S(2)}) collective-permute-start(f32[2,64,1024]{2,1,0:T(8,128)} %bitcast.22), channel_id=1, source_target_pairs={{0,32},{1,129},{32,64},{33,161},{64,96},{65,193},{96,0},{97,225},{... | collective-permute-start | bytes 1572872 | tf_op jit(solution)/shard_map/ppermute | solution.py:247
  64.4 21.4 %collective-permute-start.5 = (f32[2,64,1024]{2,1,0:T(8,128)}, f32[2,64,1024]{2,1,0:T(8,128)}, u32[]{:S(2)}, u32[]{:S(2)}) collective-permute-start(f32[2,64,1024]{2,1,0:T(8,128)} %collective-permute-done.4.refs_4_), channel_id=1, source_target_pairs={{0,2},{1,31},{2,4},{3,1},{4,6},{5,3},{6,8},{7,5},{8,10},{9,7},{10,... | collective-permute-start | bytes 1572872 | tf_op jit(solution)/shard_map/ppermute | solution.py:244
  66.4 23.4 %collective-permute-start.13 = (f32[2,64,1024]{2,1,0:T(8,128)}, f32[2,64,1024]{2,1,0:T(8,128)}, u32[]{:S(2)}, u32[]{:S(2)}) collective-permute-start(f32[2,64,1024]{2,1,0:T(8,128)} %collective-permute-done.12.refs_11_.refs_12_), channel_id=1, source_target_pairs={{0,2},{1,31},{2,4},{3,1},{4,6},{5,3},{6,8},{7,5},{8,10},{9,7},{10,... | collective-permute-start | bytes 1572872 | tf_op jit(solution)/shard_map/ppermute | solution.py:246
  69.1 13.9 %collective-permute-start = (s32[37]{0:T(128)S(1)}, s32[37]{0:T(128)S(1)}, u32[]{:S(2)}, u32[]{:S(2)}) collective-permute-start(s32[37]{0:T(128)S(1)} %concatenate.3.info), channel_id=1, source_target_pairs={{0,1},{1,0},{2,3},{3,2},{4,5},{5,4},{6,7},{7,6},{8,9},{9,8},{10,11... | collective-permute-start | bytes 452 | tf_op jit(solution)/shard_map/ppermute | solution.py:249
  75.9 49.0 %collective-permute-start.21 = (f32[4,2,64,1024]{3,2,1,0:T(8,128)S(1)}, f32[4,2,64,1024]{3,2,1,0:T(8,128)S(1)}, u32[]{:S(2)}, u32[]{:S(2)}) collective-permute-start(f32[4,2,64,1024]{3,2,1,0:T(8,128)S(1)} %pad_maximum_fusion.u0), channel_id=1, source_target_pairs={{0,128},{1,33},{32,160},{33,65},{64,192},{65,97},{96,224},{97,1},{... | collective-permute-start | bytes 6291464 | tf_op jit(solution)/shard_map/ppermute | solution.py:248
  78.4 48.8 %collective-permute-start.22 = (f32[4,2,64,1024]{3,2,1,0:T(8,128)S(1)}, f32[4,2,64,1024]{3,2,1,0:T(8,128)S(1)}, u32[]{:S(2)}, u32[]{:S(2)}) collective-permute-start(f32[4,2,64,1024]{3,2,1,0:T(8,128)S(1)} %pad_maximum_fusion.u0), channel_id=1, source_target_pairs={{0,256},{1,65},{32,288},{33,97},{64,320},{65,1},{96,352},{97,33},{... | collective-permute-start | bytes 6291464 | tf_op jit(solution)/shard_map/ppermute | solution.py:248
  83.0 46.2 %collective-permute-start.23 = (f32[4,2,64,1024]{3,2,1,0:T(8,128)S(1)}, f32[4,2,64,1024]{3,2,1,0:T(8,128)S(1)}, u32[]{:S(2)}, u32[]{:S(2)}) collective-permute-start(f32[4,2,64,1024]{3,2,1,0:T(8,128)S(1)} %pad_maximum_fusion.u0), channel_id=1, source_target_pairs={{0,384},{1,97},{32,416},{33,1},{64,448},{65,33},{96,480},{97,65},{... | collective-permute-start | bytes 6291464 | tf_op jit(solution)/shard_map/ppermute | solution.py:248
  85.9 10.4 %collective-permute-start.6 = (f32[2,64,1024]{2,1,0:T(8,128)}, f32[2,64,1024]{2,1,0:T(8,128)S(1)}, u32[]{:S(2)}, u32[]{:S(2)}) collective-permute-start(f32[2,64,1024]{2,1,0:T(8,128)} %collective-permute-done.5.refs_5_), channel_id=1, source_target_pairs={{0,2},{1,31},{2,4},{3,1},{4,6},{5,3},{6,8},{7,5},{8,10},{9,7},{10,... | collective-permute-start | bytes 1572872 | tf_op jit(solution)/shard_map/ppermute | solution.py:244
  89.8 12.1 %collective-permute-start.14 = (f32[2,64,1024]{2,1,0:T(8,128)}, f32[2,64,1024]{2,1,0:T(8,128)S(1)}, u32[]{:S(2)}, u32[]{:S(2)}) collective-permute-start(f32[2,64,1024]{2,1,0:T(8,128)} %collective-permute-done.13.refs_12_.refs_13_), channel_id=1, source_target_pairs={{0,2},{1,31},{2,4},{3,1},{4,6},{5,3},{6,8},{7,5},{8,10},{9,7},{10,... | collective-permute-start | bytes 1572872 | tf_op jit(solution)/shard_map/ppermute | solution.py:246
  96.3 16.9 %copy-start.7 = (f32[2,64,1024]{2,1,0:T(8,128)}, f32[2,64,1024]{2,1,0:T(8,128)S(1)}, u32[]{:S(2)}) copy-start(f32[2,64,1024]{2,1,0:T(8,128)S(1)} %collective-permute-done.6.refs_6_) | copy-start | bytes 1572868
  96.3 11.2 %collective-permute-start.7 = (f32[2,64,1024]{2,1,0:T(8,128)S(1)}, f32[2,64,1024]{2,1,0:T(8,128)S(1)}, u32[]{:S(2)}, u32[]{:S(2)}) collective-permute-start(f32[2,64,1024]{2,1,0:T(8,128)S(1)} %collective-permute-done.6.refs_6_), channel_id=1, source_target_pairs={{0,2},{1,31},{2,4},{3,1},{4,6},{5,3},{6,8},{7,5},{8,10},{9,7},{10,... | collective-permute-start | bytes 1572872 | tf_op jit(solution)/shard_map/ppermute | solution.py:244
  101.9 11.3 %copy-start.8 = (f32[2,64,1024]{2,1,0:T(8,128)}, f32[2,64,1024]{2,1,0:T(8,128)S(1)}, u32[]{:S(2)}) copy-start(f32[2,64,1024]{2,1,0:T(8,128)S(1)} %collective-permute-done.14.refs_13_.refs_14_) | copy-start | bytes 1572868
  101.9 11.2 %collective-permute-start.15 = (f32[2,64,1024]{2,1,0:T(8,128)S(1)}, f32[2,64,1024]{2,1,0:T(8,128)S(1)}, u32[]{:S(2)}, u32[]{:S(2)}) collective-permute-start(f32[2,64,1024]{2,1,0:T(8,128)S(1)} %collective-permute-done.14.refs_13_.refs_14_), channel_id=1, source_target_pairs={{0,2},{1,31},{2,4},{3,1},{4,6},{5,3},{6,8},{7,5},{8,10},{9,7},{10,... | collective-permute-start | bytes 1572872 | tf_op jit(solution)/shard_map/ppermute | solution.py:246
  115.0 35.6 %copy-start = (f32[1,1,2,64,1024]{4,3,2,1,0:T(8,128)S(1)}, f32[1,1,2,64,1024]{4,3,2,1,0:T(8,128)}, u32[]{:S(2)}) copy-start(f32[1,1,2,64,1024]{4,3,2,1,0:T(8,128)} %param.11) | copy-start | bytes 1572868
  115.0 38.4 %collective-permute-start.16 = (f32[4,2,64,1024]{3,2,1,0:T(8,128)S(1)}, f32[4,2,64,1024]{3,2,1,0:T(8,128)S(1)}, u32[]{:S(2)}, u32[]{:S(2)}) collective-permute-start(f32[4,2,64,1024]{3,2,1,0:T(8,128)S(1)} %shard_map.77), channel_id=1, source_target_pairs={{0,1},{1,0},{2,3},{3,2},{4,5},{5,4},{6,7},{7,6},{8,9},{9,8},{10,11... | collective-permute-start | bytes 6291464 | tf_op jit(solution)/shard_map/ppermute | solution.py:268
  130.1 20.5 %collective-permute-start.24 = (f32[2,2,64,1024]{3,2,1,0:T(8,128)S(1)}, f32[2,2,64,1024]{3,2,1,0:T(8,128)S(1)}, u32[]{:S(2)}, u32[]{:S(2)}) collective-permute-start(f32[2,2,64,1024]{3,2,1,0:T(8,128)S(1)} %get-tuple-element.13), channel_id=1, source_target_pairs={{0,1},{1,0},{2,3},{3,2},{4,5},{5,4},{6,7},{7,6},{8,9},{9,8},{10,11... | collective-permute-start | bytes 3145736 | tf_op jit(solution)/shard_map/ppermute | solution.py:266
  136.3 11.0 %collective-permute-start.8 = (f32[2,64,1024]{2,1,0:T(8,128)S(1)}, f32[2,64,1024]{2,1,0:T(8,128)S(1)}, u32[]{:S(2)}, u32[]{:S(2)}) collective-permute-start(f32[2,64,1024]{2,1,0:T(8,128)S(1)} %collective-permute-done.7.refs_7_), channel_id=1, source_target_pairs={{0,2},{1,31},{2,4},{3,1},{4,6},{5,3},{6,8},{7,5},{8,10},{9,7},{10,... | collective-permute-start | bytes 1572872 | tf_op jit(solution)/shard_map/ppermute | solution.py:244
  147.3 6.1 %collective-permute-start.17 = (f32[2,64,1024]{2,1,0:T(8,128)S(1)}, f32[2,64,1024]{2,1,0:T(8,128)S(1)}, u32[]{:S(2)}, u32[]{:S(2)}) collective-permute-start(f32[2,64,1024]{2,1,0:T(8,128)S(1)} %collective-permute-done.8.refs_8_), channel_id=1, source_target_pairs={{0,1},{1,0},{2,3},{3,2},{4,5},{5,4},{6,7},{7,6},{8,9},{9,8},{10,11... | collective-permute-start | bytes 1572872 | tf_op jit(solution)/shard_map/ppermute | solution.py:269
where the time goes:
time: 161 us; the launch traced here: 160 us
  starting transfers between devices  113 us (70%)
  waiting for transfers between devices  31.4 us (20%)
  Pallas kernels  12.4 us (8%)
  other arithmetic  1.65 us (1%)
    ppermute x8, starting transfers between devices, pieces_and_tile(): own_pieces.append(lax.ppermute(own_pieces[-1], axes, shift))  42.7 us
    ppermute x6, starting transfers between devices, pieces_and_tile(): across_pieces.append(lax.ppermute(across_pieces[-1], axes, shift))  23.9 us
    ppermute x8, waiting for transfers between devices, pieces_and_tile(): own_pieces.append(lax.ppermute(own_pieces[-1], axes, shift))  19.8 us
    ppermute x3, starting transfers between devices, pieces_and_tile(): lax.ppermute(up, ('row', 'depth'), xy_shift(s, 0))  10.1 us
    ppermute x3, starting transfers between devices, pieces_and_tile(): lax.ppermute(block, ('row', 'depth'), xy_shift(s, 1))  9.91 us
    ppermute x1, starting transfers between devices, pieces_and_tile(): lax.ppermute(left_choice(info, other, *own_held[:8], *across_held)[0], 'd...  9.85 us
    ppermute x6, waiting for transfers between devices, pieces_and_tile(): across_pieces.append(lax.ppermute(across_pieces[-1], axes, shift))  7.29 us
    pallas_call x1, Pallas kernels, pieces_and_tile(): whole(info, other, *own_held, *across_held, left_in, last_in, *sides)  6.89 us
  transfers between devices with their start and end apart: 25, of which 12 were waited for; matrix products, arithmetic and copies ran while one was open for 2% of the time, Pallas kernels for 3%

commit v1 on v0

--- a/solution.py
+++ b/solution.py
@@ -54,7 +54,7 @@
         drawn[k] = dot(tested[:, k * n : k * n + n], ps[k], (1, 0))
 
 
-def up_kernel(info, u0, u1, u2, u3, out, ps, qs, sems, own_sems):
+def up_kernel(info, u0, u1, u2, u3, sketch, out, ps, qs, drawn, ws, sems, own_sems, sketch_sem):
     ups = (u0, u1, u2, u3)
     depth = info[DEPTH_AT]
     j_own, j_other = info[TARGET_AT + depth] % CB, info[TARGET_AT + 1 - depth] % CB
@@ -65,6 +65,7 @@
             pltpu.make_async_copy(source.at[0], ps.at[k], own_sems.at[k, 0]),
         )
 
+    pltpu.make_async_copy(sketch.at[depth], ws, sketch_sem).start()
     for k in range(KD):
         t, s = up_place(info, info[UP_AT + j_other * KD + k])
         t_own, s_own = up_place(info, info[UP_AT + j_own * KD + k])
@@ -79,9 +80,11 @@
                 for copy in copies(ups[i].at[s_own], k):
                     copy.start()
 
+    pltpu.make_async_copy(sketch.at[0], ws, sketch_sem).wait()
     for k in range(KD):
         for copy in copies(u0.at[0], k):
             copy.wait()
+    draw(ws, ps, qs, drawn)
     for k in range(KD):
         pltpu.make_async_copy(u0.at[0], out.at[k], sems.at[k]).wait()
 
@@ -163,14 +166,12 @@
     return jnp.concatenate(blocks, axis=0)[:, n:]
 
 
-def across_kernel(info, up_in, sketch, ps_own, qs_own, ps, qs, drawn_own, drawn, ws, sems, sketch_sem):
+def across_kernel(info, up_in, sketch, ps, qs, drawn, ws, sems, sketch_sem):
     sketch_copy = pltpu.make_async_copy(sketch.at[info[DEPTH_AT]], ws, sketch_sem)
     copies = [pltpu.make_async_copy(up_in.at[k, 1 - i], (qs, ps)[i].at[k], sems.at[k, i]) for k in range(KD) for i in range(2)]
     for copy in (sketch_copy, *copies):
         copy.start()
-    sketch_copy.wait()
-    draw(ws, ps_own, qs_own, drawn_own)
-    for copy in copies:
+    for copy in (sketch_copy, *copies):
         copy.wait()
     draw(ws, ps, qs, drawn)
 
@@ -259,19 +260,18 @@
     tile, couple = array(*flat), array(KD, *flat)
     tile_scratch = vmem(flat, f32)
 
-    outs = array(KD, *pair), couple, couple
-    scratch = [dma((KD,)), dma((KD, 2))]
-    up_part = local_kernel(up_kernel, [smem] + [hbm] * SIDE, outs, [hbm] + [vmem] * 2, scratch, 6)
-    choice, p_own, q_own = up_part(info, *ups)
+    outs = array(KD, *pair), couple, couple, couple
+    scratch = [tile_scratch, dma((KD,)), dma((KD, 2)), dma]
+    up_part = local_kernel(up_kernel, [smem] + [hbm] * (SIDE + 1), outs, [hbm] + [vmem] * 3, scratch, 6)
+    choice, p_own, q_own, drawn_own = up_part(info, *ups, test)
     up_in = lax.ppermute(choice, "depth", SWAP)
     left_choice = local_kernel(left_choice_kernel, [smem] * 2 + [hbm] * 15, (array(slots, *pair),), [hbm], [dma((slots,))])
     left_in = lax.ppermute(left_choice(info, other, *own_held[:8], *across_held)[0], "depth", SWAP)
     last_in = lax.ppermute(own_pieces[8], "depth", SWAP)
 
     scratch = [tile_scratch, dma((KD, 2)), dma]
-    across_part = local_kernel(across_kernel, [smem] + [hbm] * 2 + [vmem] * 2, (couple,) * 4, [vmem] * 4, scratch, 6)
-    p_across, q_across, drawn_own, drawn_across = across_part(info, up_in, test, p_own, q_own)
-    sides = p_own, q_own, drawn_own, p_across, q_across, drawn_across
+    across_part = local_kernel(across_kernel, [smem] + [hbm] * 2, (couple, couple, couple), [vmem] * 3, scratch, 4)
+    sides = p_own, q_own, drawn_own, *across_part(info, up_in, test)
     scratch = [vmem((slots, *pair), f32)] + [tile_scratch] * 2 + [dma((slots,)), dma((5,))]
     whole = local_kernel(tile_kernel, [smem] * 2 + [hbm] * 18 + [vmem] * 6, (tile, tile), [hbm] * 2, scratch, 12)
     basis, weights = whole(info, other, *own_held, *across_held, left_in, last_in, *sides)

time: 161 us -> 162 us (level)
  no operation moved by 1% of the time
where the time goes in v1:
time: 162 us; the launch traced here: 161 us
  starting transfers between devices  113 us (70%)
  waiting for transfers between devices  31.5 us (19%)
  Pallas kernels  12.5 us (8%)
  other arithmetic  1.65 us (1%)
    ppermute x8, starting transfers between devices, pieces_and_tile(): own_pieces.append(lax.ppermute(own_pieces[-1], axes, shift))  42.7 us
    ppermute x6, starting transfers between devices, pieces_and_tile(): across_pieces.append(lax.ppermute(across_pieces[-1], axes, shift))  23.9 us
    ppermute x8, waiting for transfers between devices, pieces_and_tile(): own_pieces.append(lax.ppermute(own_pieces[-1], axes, shift))  19.8 us
    ppermute x3, starting transfers between devices, pieces_and_tile(): lax.ppermute(up, ('row', 'depth'), xy_shift(s, 0))  10.1 us
    ppermute x3, starting transfers between devices, pieces_and_tile(): lax.ppermute(block, ('row', 'depth'), xy_shift(s, 1))  10 us
    ppermute x1, starting transfers between devices, pieces_and_tile(): lax.ppermute(left_choice(info, other, *own_held[:8], *across_held)[0], 'd...  9.71 us
    ppermute x6, waiting for transfers between devices, pieces_and_tile(): across_pieces.append(lax.ppermute(across_pieces[-1], axes, shift))  7.29 us
    pallas_call x1, Pallas kernels, pieces_and_tile(): whole(info, other, *own_held, *across_held, left_in, last_in, *sides)  6.89 us
  transfers between devices with their start and end apart: 25, of which 12 were waited for; matrix products, arithmetic and copies ran while one was open for 2% of the time, Pallas kernels for 3%

profile of v1, /device:TPU:1, one launch (start us, length us, event | category | flops | bytes accessed | tf_op | source)
XLA Modules:
  0.0 160.5 jit_solution(3890261595162730739)
XLA Ops:
  0.6 11.9 %collective-permute-start.1 = (f32[2,64,1024]{2,1,0:T(8,128)}, f32[2,64,1024]{2,1,0:T(8,128)S(1)}, u32[]{:S(2)}, u32[]{:S(2)}) collective-permute-start(f32[2,64,1024]{2,1,0:T(8,128)} %bitcast.17), channel_id=1, source_target_pairs={{0,2},{1,31},{2,4},{3,1},{4,6},{5,3},{6,8},{7,5},{8,10},{9,7},{10,... | collective-permute-start | bytes 1572872 | tf_op jit(solution)/shard_map/ppermute | solution.py:245
  12.6 1.9 %collective-permute-start.9 = (f32[2,64,1024]{2,1,0:T(8,128)}, f32[2,64,1024]{2,1,0:T(8,128)S(1)}, u32[]{:S(2)}, u32[]{:S(2)}) collective-permute-start(f32[2,64,1024]{2,1,0:T(8,128)} %bitcast.18), channel_id=1, source_target_pairs={{1,2},{0,31},{3,4},{2,1},{5,6},{4,3},{7,8},{6,5},{9,10},{8,7},{11,... | collective-permute-start | bytes 1572872 | tf_op jit(solution)/shard_map/ppermute | solution.py:243
  14.5 6.9 %collective-permute-done.1.refs_1_ = f32[2,64,1024]{2,1,0:T(8,128)S(1)} collective-permute-done((f32[2,64,1024]{2,1,0:T(8,128)}, f32[2,64,1024]{2,1,0:T(8,128)S(1)}, u32[]{:S(2)}, u32[]{:S(2)}) %collective-permute-start.1) | collective-permute-done | bytes 524320 | tf_op jit(solution)/shard_map/ppermute | solution.py:245
  21.4 4.9 %collective-permute-start.2 = (f32[2,64,1024]{2,1,0:T(8,128)S(1)}, f32[2,64,1024]{2,1,0:T(8,128)S(1)}, u32[]{:S(2)}, u32[]{:S(2)}) collective-permute-start(f32[2,64,1024]{2,1,0:T(8,128)S(1)} %collective-permute-done.1.refs_1_), channel_id=1, source_target_pairs={{0,2},{1,31},{2,4},{3,1},{4,6},{5,3},{6,8},{7,5},{8,10},{9,7},{10,... | collective-permute-start | bytes 1572872 | tf_op jit(solution)/shard_map/ppermute | solution.py:245
  26.3 0.0 collective-permute-done.9.refs_8_.refs_9_
  26.3 0.0 copy-start.2
  26.3 3.2 %collective-permute-start.10 = (f32[2,64,1024]{2,1,0:T(8,128)S(1)}, f32[2,64,1024]{2,1,0:T(8,128)S(1)}, u32[]{:S(2)}, u32[]{:S(2)}) collective-permute-start(f32[2,64,1024]{2,1,0:T(8,128)S(1)} %collective-permute-done.9.refs_8_.refs_9_), channel_id=1, source_target_pairs={{0,2},{1,31},{2,4},{3,1},{4,6},{5,3},{6,8},{7,5},{8,10},{9,7},{10,... | collective-permute-start | bytes 1572872 | tf_op jit(solution)/shard_map/ppermute | solution.py:247
  29.5 2.9 %collective-permute-done.2.refs_2_ = f32[2,64,1024]{2,1,0:T(8,128)S(1)} collective-permute-done((f32[2,64,1024]{2,1,0:T(8,128)S(1)}, f32[2,64,1024]{2,1,0:T(8,128)S(1)}, u32[]{:S(2)}, u32[]{:S(2)}) %collective-permute-start.2) | collective-permute-done | bytes 524320 | tf_op jit(solution)/shard_map/ppermute | solution.py:245
  32.4 5.0 %collective-permute-start.3 = (f32[2,64,1024]{2,1,0:T(8,128)S(1)}, f32[2,64,1024]{2,1,0:T(8,128)S(1)}, u32[]{:S(2)}, u32[]{:S(2)}) collective-permute-start(f32[2,64,1024]{2,1,0:T(8,128)S(1)} %collective-permute-done.2.refs_2_), channel_id=1, source_target_pairs={{0,2},{1,31},{2,4},{3,1},{4,6},{5,3},{6,8},{7,5},{8,10},{9,7},{10,... | collective-permute-start | bytes 1572872 | tf_op jit(solution)/shard_map/ppermute | solution.py:245
  37.4 0.6 collective-permute-done.10.refs_9_.refs_10_
  38.0 5.0 %collective-permute-start.11 = (f32[2,64,1024]{2,1,0:T(8,128)S(1)}, f32[2,64,1024]{2,1,0:T(8,128)S(1)}, u32[]{:S(2)}, u32[]{:S(2)}) collective-permute-start(f32[2,64,1024]{2,1,0:T(8,128)S(1)} %collective-permute-done.10.refs_9_.refs_10_), channel_id=1, source_target_pairs={{0,2},{1,31},{2,4},{3,1},{4,6},{5,3},{6,8},{7,5},{8,10},{9,7},{10,... | collective-permute-start | bytes 1572872 | tf_op jit(solution)/shard_map/ppermute | solution.py:247
  43.1 0.6 collective-permute-done.3.refs_3_
  43.7 5.0 %collective-permute-start.4 = (f32[2,64,1024]{2,1,0:T(8,128)S(1)}, f32[2,64,1024]{2,1,0:T(8,128)}, u32[]{:S(2)}, u32[]{:S(2)}) collective-permute-start(f32[2,64,1024]{2,1,0:T(8,128)S(1)} %collective-permute-done.3.refs_3_), channel_id=1, source_target_pairs={{0,2},{1,31},{2,4},{3,1},{4,6},{5,3},{6,8},{7,5},{8,10},{9,7},{10,... | collective-permute-start | bytes 1572872 | tf_op jit(solution)/shard_map/ppermute | solution.py:245
  48.7 0.6 collective-permute-done.11.refs_10_.refs_11_
  49.3 5.0 %collective-permute-start.12 = (f32[2,64,1024]{2,1,0:T(8,128)S(1)}, f32[2,64,1024]{2,1,0:T(8,128)}, u32[]{:S(2)}, u32[]{:S(2)}) collective-permute-start(f32[2,64,1024]{2,1,0:T(8,128)S(1)} %collective-permute-done.11.refs_10_.refs_11_), channel_id=1, source_target_pairs={{0,2},{1,31},{2,4},{3,1},{4,6},{5,3},{6,8},{7,5},{8,10},{9,7},{10,... | collective-permute-start | bytes 1572872 | tf_op jit(solution)/shard_map/ppermute | solution.py:247
  54.3 4.8 %collective-permute-start.19 = (f32[2,64,1024]{2,1,0:T(8,128)}, f32[2,64,1024]{2,1,0:T(8,128)}, u32[]{:S(2)}, u32[]{:S(2)}) collective-permute-start(f32[2,64,1024]{2,1,0:T(8,128)} %bitcast.21), channel_id=1, source_target_pairs={{0,64},{1,257},{32,96},{33,289},{64,0},{65,321},{96,32},{97,353},{... | collective-permute-start | bytes 1572872 | tf_op jit(solution)/shard_map/ppermute | solution.py:248
  59.1 2.7 %collective-permute-start.20 = (f32[2,64,1024]{2,1,0:T(8,128)}, f32[2,64,1024]{2,1,0:T(8,128)}, u32[]{:S(2)}, u32[]{:S(2)}) collective-permute-start(f32[2,64,1024]{2,1,0:T(8,128)} %bitcast.22), channel_id=1, source_target_pairs={{0,96},{1,385},{32,0},{33,417},{64,32},{65,449},{96,64},{97,481},{... | collective-permute-start | bytes 1572872 | tf_op jit(solution)/shard_map/ppermute | solution.py:248
  61.8 2.6 %collective-permute-start.18 = (f32[2,64,1024]{2,1,0:T(8,128)}, f32[2,64,1024]{2,1,0:T(8,128)}, u32[]{:S(2)}, u32[]{:S(2)}) collective-permute-start(f32[2,64,1024]{2,1,0:T(8,128)} %bitcast.23), channel_id=1, source_target_pairs={{0,32},{1,129},{32,64},{33,161},{64,96},{65,193},{96,0},{97,225},{... | collective-permute-start | bytes 1572872 | tf_op jit(solution)/shard_map/ppermute | solution.py:248
  64.4 0.0 collective-permute-done.4.refs_4_
  64.4 1.9 %collective-permute-start.5 = (f32[2,64,1024]{2,1,0:T(8,128)}, f32[2,64,1024]{2,1,0:T(8,128)}, u32[]{:S(2)}, u32[]{:S(2)}) collective-permute-start(f32[2,64,1024]{2,1,0:T(8,128)} %collective-permute-done.4.refs_4_), channel_id=1, source_target_pairs={{0,2},{1,31},{2,4},{3,1},{4,6},{5,3},{6,8},{7,5},{8,10},{9,7},{10,... | collective-permute-start | bytes 1572872 | tf_op jit(solution)/shard_map/ppermute | solution.py:245
  66.4 0.0 collective-permute-done.12.refs_11_.refs_12_
  66.4 1.9 %collective-permute-start.13 = (f32[2,64,1024]{2,1,0:T(8,128)}, f32[2,64,1024]{2,1,0:T(8,128)}, u32[]{:S(2)}, u32[]{:S(2)}) collective-permute-start(f32[2,64,1024]{2,1,0:T(8,128)} %collective-permute-done.12.refs_11_.refs_12_), channel_id=1, source_target_pairs={{0,2},{1,31},{2,4},{3,1},{4,6},{5,3},{6,8},{7,5},{8,10},{9,7},{10,... | collective-permute-start | bytes 1572872 | tf_op jit(solution)/shard_map/ppermute | solution.py:247
  68.3 0.8 concatenate.3.info
  69.1 0.0 collective-permute-done.19
  69.1 5.1 %collective-permute-start = (s32[37]{0:T(128)S(1)}, s32[37]{0:T(128)S(1)}, u32[]{:S(2)}, u32[]{:S(2)}) collective-permute-start(s32[37]{0:T(128)S(1)} %concatenate.3.info), channel_id=1, source_target_pairs={{0,1},{1,0},{2,3},{3,2},{4,5},{5,4},{6,7},{7,6},{8,9},{9,8},{10,11... | collective-permute-start | bytes 452 | tf_op jit(solution)/shard_map/ppermute | solution.py:250
  74.2 0.0 collective-permute-done.20
  74.2 0.0 collective-permute-done.18
  74.2 1.7 %pad_maximum_fusion.u0 = f32[4,2,64,1024]{3,2,1,0:T(8,128)S(1)} fusion(f32[1,2,64,1024]{3,2,1,0:T(8,128)} %bitcast.11, f32[1,2,64,1024]{3,2,1,0:T(8,128)} %bitcast.10, f32[1,2,64,1024]{3,2,1,0:T(8,128)} %bitcast.9, f32[1,2,64,1024]{3,2,1,0:T(8,128)} %bitcast.24), kind=kLoop, calls=%fused_computation | loop fusion | flops 1572864 | bytes 4194304 | tf_op jit(solution)/shard_map/stack | solution.py:248
  75.9 0.0 copy-done.1
  75.9 0.0 copy-done.2
  75.9 0.0 copy-done.3
  75.9 0.0 copy-done.4
  75.9 0.0 copy-done.5
  75.9 0.0 copy-start
  75.9 2.6 %collective-permute-start.21 = (f32[4,2,64,1024]{3,2,1,0:T(8,128)S(1)}, f32[4,2,64,1024]{3,2,1,0:T(8,128)S(1)}, u32[]{:S(2)}, u32[]{:S(2)}) collective-permute-start(f32[4,2,64,1024]{3,2,1,0:T(8,128)S(1)} %pad_maximum_fusion.u0), channel_id=1, source_target_pairs={{0,128},{1,33},{32,160},{33,65},{64,192},{65,97},{96,224},{97,1},{... | collective-permute-start | bytes 6291464 | tf_op jit(solution)/shard_map/ppermute | solution.py:249
  78.6 4.6 %collective-permute-start.22 = (f32[4,2,64,1024]{3,2,1,0:T(8,128)S(1)}, f32[4,2,64,1024]{3,2,1,0:T(8,128)S(1)}, u32[]{:S(2)}, u32[]{:S(2)}) collective-permute-start(f32[4,2,64,1024]{3,2,1,0:T(8,128)S(1)} %pad_maximum_fusion.u0), channel_id=1, source_target_pairs={{0,256},{1,65},{32,288},{33,97},{64,320},{65,1},{96,352},{97,33},{... | collective-permute-start | bytes 6291464 | tf_op jit(solution)/shard_map/ppermute | solution.py:249
  83.1 0.0 collective-permute-done.other
  83.2 2.8 %collective-permute-start.23 = (f32[4,2,64,1024]{3,2,1,0:T(8,128)S(1)}, f32[4,2,64,1024]{3,2,1,0:T(8,128)S(1)}, u32[]{:S(2)}, u32[]{:S(2)}) collective-permute-start(f32[4,2,64,1024]{3,2,1,0:T(8,128)S(1)} %pad_maximum_fusion.u0), channel_id=1, source_target_pairs={{0,384},{1,97},{32,416},{33,1},{64,448},{65,33},{96,480},{97,65},{... | collective-permute-start | bytes 6291464 | tf_op jit(solution)/shard_map/ppermute | solution.py:249
  86.0 0.0 collective-permute-done.5.refs_5_
  86.0 3.9 %collective-permute-start.6 = (f32[2,64,1024]{2,1,0:T(8,128)}, f32[2,64,1024]{2,1,0:T(8,128)S(1)}, u32[]{:S(2)}, u32[]{:S(2)}) collective-permute-start(f32[2,64,1024]{2,1,0:T(8,128)} %collective-permute-done.5.refs_5_), channel_id=1, source_target_pairs={{0,2},{1,31},{2,4},{3,1},{4,6},{5,3},{6,8},{7,5},{8,10},{9,7},{10,... | collective-permute-start | bytes 1572872 | tf_op jit(solution)/shard_map/ppermute | solution.py:245
  90.0 0.0 collective-permute-done.13.refs_12_.refs_13_
  90.0 3.6 %collective-permute-start.14 = (f32[2,64,1024]{2,1,0:T(8,128)}, f32[2,64,1024]{2,1,0:T(8,128)S(1)}, u32[]{:S(2)}, u32[]{:S(2)}) collective-permute-start(f32[2,64,1024]{2,1,0:T(8,128)} %collective-permute-done.13.refs_12_.refs_13_), channel_id=1, source_target_pairs={{0,2},{1,31},{2,4},{3,1},{4,6},{5,3},{6,8},{7,5},{8,10},{9,7},{10,... | collective-permute-start | bytes 1572872 | tf_op jit(solution)/shard_map/ppermute | solution.py:247
  93.6 2.8 %collective-permute-done.6.refs_6_ = f32[2,64,1024]{2,1,0:T(8,128)S(1)} collective-permute-done((f32[2,64,1024]{2,1,0:T(8,128)}, f32[2,64,1024]{2,1,0:T(8,128)S(1)}, u32[]{:S(2)}, u32[]{:S(2)}) %collective-permute-start.6) | collective-permute-done | bytes 524320 | tf_op jit(solution)/shard_map/ppermute | solution.py:245
  96.4 5.1 %collective-permute-start.7 = (f32[2,64,1024]{2,1,0:T(8,128)S(1)}, f32[2,64,1024]{2,1,0:T(8,128)S(1)}, u32[]{:S(2)}, u32[]{:S(2)}) collective-permute-start(f32[2,64,1024]{2,1,0:T(8,128)S(1)} %collective-permute-done.6.refs_6_), channel_id=1, source_target_pairs={{0,2},{1,31},{2,4},{3,1},{4,6},{5,3},{6,8},{7,5},{8,10},{9,7},{10,... | collective-permute-start | bytes 1572872 | tf_op jit(solution)/shard_map/ppermute | solution.py:245
  101.6 0.5 collective-permute-done.14.refs_13_.refs_14_
  102.1 5.1 %collective-permute-start.15 = (f32[2,64,1024]{2,1,0:T(8,128)S(1)}, f32[2,64,1024]{2,1,0:T(8,128)S(1)}, u32[]{:S(2)}, u32[]{:S(2)}) collective-permute-start(f32[2,64,1024]{2,1,0:T(8,128)S(1)} %collective-permute-done.14.refs_13_.refs_14_), channel_id=1, source_target_pairs={{0,2},{1,31},{2,4},{3,1},{4,6},{5,3},{6,8},{7,5},{8,10},{9,7},{10,... | collective-permute-start | bytes 1572872 | tf_op jit(solution)/shard_map/ppermute | solution.py:247
  107.2 0.5 collective-permute-done.7.refs_7_
  107.7 5.6 %collective-permute-done.15.refs_14_.refs_15_ = f32[2,64,1024]{2,1,0:T(8,128)S(1)} collective-permute-done((f32[2,64,1024]{2,1,0:T(8,128)S(1)}, f32[2,64,1024]{2,1,0:T(8,128)S(1)}, u32[]{:S(2)}, u32[]{:S(2)}) %collective-permute-start.15) | collective-permute-done | bytes 524320 | tf_op jit(solution)/shard_map/ppermute | solution.py:247
  113.3 0.0 copy-done.8
  113.3 1.8 %shard_map.77 = f32[4,2,64,1024]{3,2,1,0:T(8,128)S(1)} custom-call(s32[37]{0:T(128)S(1)} %concatenate.3.info, s32[37]{0:T(128)S(1)} %collective-permute-done.other, f32[2,64,1024]{2,1,0:T(8,128)} %bitcast.19, f32[2,64,1024]{2,1,0:T(8,128)} %copy-done.1, f32[2,64,1024]{2,1,0:T(8,128)} %copy-done.3, f32[2,64,1024]{2,1,0:T(8,128)} %copy-done.5, ...), custom_call_target="tpu_custom_call" | custom-call | tf_op jit(solution)/shard_map/pallas_call | solution.py:269
  115.2 9.7 %collective-permute-start.16 = (f32[4,2,64,1024]{3,2,1,0:T(8,128)S(1)}, f32[4,2,64,1024]{3,2,1,0:T(8,128)S(1)}, u32[]{:S(2)}, u32[]{:S(2)}) collective-permute-start(f32[4,2,64,1024]{3,2,1,0:T(8,128)S(1)} %shard_map.77), channel_id=1, source_target_pairs={{0,1},{1,0},{2,3},{3,2},{4,5},{5,4},{6,7},{7,6},{8,9},{9,8},{10,11... | collective-permute-start | bytes 6291464 | tf_op jit(solution)/shard_map/ppermute | solution.py:269
  124.9 0.0 collective-permute-done.21.u1
  124.9 2.5 %collective-permute-done.22.u2 = f32[4,2,64,1024]{3,2,1,0:T(8,128)S(1)} collective-permute-done((f32[4,2,64,1024]{3,2,1,0:T(8,128)S(1)}, f32[4,2,64,1024]{3,2,1,0:T(8,128)S(1)}, u32[]{:S(2)}, u32[]{:S(2)}) %collective-permute-start.22) | collective-permute-done | bytes 2097184 | tf_op jit(solution)/shard_map/ppermute | solution.py:249
  127.4 2.0 %collective-permute-done.23.u3 = f32[4,2,64,1024]{3,2,1,0:T(8,128)S(1)} collective-permute-done((f32[4,2,64,1024]{3,2,1,0:T(8,128)S(1)}, f32[4,2,64,1024]{3,2,1,0:T(8,128)S(1)}, u32[]{:S(2)}, u32[]{:S(2)}) %collective-permute-start.23) | collective-permute-done | bytes 2097184 | tf_op jit(solution)/shard_map/ppermute | solution.py:249
  129.4 2.0 %shard_map.78 = (f32[2,2,64,1024]{3,2,1,0:T(8,128)S(1)}, f32[2,64,1024]{2,1,0:T(8,128)S(1)}, f32[2,64,1024]{2,1,0:T(8,128)S(1)}, f32[2,64,1024]{2,1,0:T(8,128)S(1)}) custom-call(s32[37]{0:T(128)S(1)} %concatenate.3.info, f32[4,2,64,1024]{3,2,1,0:T(8,128)S(1)} %pad_maximum_fusion.u0, f32[4,2,64,1024]{3,2,1,0:T(8,128)S(1)} %collective-permute-done.21.u1, ...), custom_call_target="tpu_custom_call" | custom-call | tf_op jit(solution)/shard_map/pallas_call | solution.py:266
  131.3 6.3 %collective-permute-start.24 = (f32[2,2,64,1024]{3,2,1,0:T(8,128)S(1)}, f32[2,2,64,1024]{3,2,1,0:T(8,128)S(1)}, u32[]{:S(2)}, u32[]{:S(2)}) collective-permute-start(f32[2,2,64,1024]{3,2,1,0:T(8,128)S(1)} %get-tuple-element.14), channel_id=1, source_target_pairs={{0,1},{1,0},{2,3},{3,2},{4,5},{5,4},{6,7},{7,6},{8,9},{9,8},{10,11... | collective-permute-start | bytes 3145736 | tf_op jit(solution)/shard_map/ppermute | solution.py:267
  137.6 4.8 %collective-permute-start.8 = (f32[2,64,1024]{2,1,0:T(8,128)S(1)}, f32[2,64,1024]{2,1,0:T(8,128)S(1)}, u32[]{:S(2)}, u32[]{:S(2)}) collective-permute-start(f32[2,64,1024]{2,1,0:T(8,128)S(1)} %collective-permute-done.7.refs_7_), channel_id=1, source_target_pairs={{0,2},{1,31},{2,4},{3,1},{4,6},{5,3},{6,8},{7,5},{8,10},{9,7},{10,... | collective-permute-start | bytes 1572872 | tf_op jit(solution)/shard_map/ppermute | solution.py:245
  142.5 6.1 %collective-permute-done.8.refs_8_ = f32[2,64,1024]{2,1,0:T(8,128)S(1)} collective-permute-done((f32[2,64,1024]{2,1,0:T(8,128)S(1)}, f32[2,64,1024]{2,1,0:T(8,128)S(1)}, u32[]{:S(2)}, u32[]{:S(2)}) %collective-permute-start.8) | collective-permute-done | bytes 524320 | tf_op jit(solution)/shard_map/ppermute | solution.py:245
  148.6 3.2 %collective-permute-start.17 = (f32[2,64,1024]{2,1,0:T(8,128)S(1)}, f32[2,64,1024]{2,1,0:T(8,128)S(1)}, u32[]{:S(2)}, u32[]{:S(2)}) collective-permute-start(f32[2,64,1024]{2,1,0:T(8,128)S(1)} %collective-permute-done.8.refs_8_), channel_id=1, source_target_pairs={{0,1},{1,0},{2,3},{3,2},{4,5},{5,4},{6,7},{7,6},{8,9},{9,8},{10,11... | collective-permute-start | bytes 1572872 | tf_op jit(solution)/shard_map/ppermute | solution.py:270
  151.8 0.0 collective-permute-done.24.up_in
  151.8 1.8 %shard_map.79 = (f32[2,64,1024]{2,1,0:T(8,128)S(1)}, f32[2,64,1024]{2,1,0:T(8,128)S(1)}, f32[2,64,1024]{2,1,0:T(8,128)S(1)}) custom-call(s32[37]{0:T(128)S(1)} %concatenate.3.info, f32[2,2,64,1024]{3,2,1,0:T(8,128)S(1)} %collective-permute-done.24.up_in, f32[2,64,1024]{2,1,0:T(8,128)S(1)} %bitcast.16), custom_call_target="tpu_custom_call" | custom-call | tf_op jit(solution)/shard_map/pallas_call | solution.py:274
  153.6 0.0 collective-permute-done.17.refs_17_
  153.6 0.0 collective-permute-done.16.refs_16_
  153.6 6.9 %shard_map.80 = (f32[64,1024]{1,0:T(8,128)}, f32[64,1024]{1,0:T(8,128)}) custom-call(s32[37]{0:T(128)S(1)} %concatenate.3.info, s32[37]{0:T(128)S(1)} %collective-permute-done.other, f32[2,64,1024]{2,1,0:T(8,128)} %bitcast.20, f32[2,64,1024]{2,1,0:T(8,128)} %copy-done.1, f32[2,64,1024]{2,1,0:T(8,128)} %copy-done.3, f32[2,64,1024]{2,1,0:T(8,128)} %copy-done.5, ...), custom_call_target="tpu_custom_call" | custom-call | tf_op jit(solution)/shard_map/pallas_call | solution.py:277
  (10 shorter events, 0.0 us)
Async XLA Ops:
  0.6 20.8 %collective-permute-start.1 = (f32[2,64,1024]{2,1,0:T(8,128)}, f32[2,64,1024]{2,1,0:T(8,128)S(1)}, u32[]{:S(2)}, u32[]{:S(2)}) collective-permute-start(f32[2,64,1024]{2,1,0:T(8,128)} %bitcast.17), channel_id=1, source_target_pairs={{0,2},{1,31},{2,4},{3,1},{4,6},{5,3},{6,8},{7,5},{8,10},{9,7},{10,... | collective-permute-start | bytes 1572872 | tf_op jit(solution)/shard_map/ppermute | solution.py:245
  12.6 13.7 %collective-permute-start.9 = (f32[2,64,1024]{2,1,0:T(8,128)}, f32[2,64,1024]{2,1,0:T(8,128)S(1)}, u32[]{:S(2)}, u32[]{:S(2)}) collective-permute-start(f32[2,64,1024]{2,1,0:T(8,128)} %bitcast.18), channel_id=1, source_target_pairs={{1,2},{0,31},{3,4},{2,1},{5,6},{4,3},{7,8},{6,5},{9,10},{8,7},{11,... | collective-permute-start | bytes 1572872 | tf_op jit(solution)/shard_map/ppermute | solution.py:243
  21.4 54.5 %copy-start.1 = (f32[2,64,1024]{2,1,0:T(8,128)}, f32[2,64,1024]{2,1,0:T(8,128)S(1)}, u32[]{:S(2)}) copy-start(f32[2,64,1024]{2,1,0:T(8,128)S(1)} %collective-permute-done.1.refs_1_) | copy-start | bytes 1572868
  21.4 11.0 %collective-permute-start.2 = (f32[2,64,1024]{2,1,0:T(8,128)S(1)}, f32[2,64,1024]{2,1,0:T(8,128)S(1)}, u32[]{:S(2)}, u32[]{:S(2)}) collective-permute-start(f32[2,64,1024]{2,1,0:T(8,128)S(1)} %collective-permute-done.1.refs_1_), channel_id=1, source_target_pairs={{0,2},{1,31},{2,4},{3,1},{4,6},{5,3},{6,8},{7,5},{8,10},{9,7},{10,... | collective-permute-start | bytes 1572872 | tf_op jit(solution)/shard_map/ppermute | solution.py:245
  26.3 49.5 %copy-start.2 = (f32[2,64,1024]{2,1,0:T(8,128)}, f32[2,64,1024]{2,1,0:T(8,128)S(1)}, u32[]{:S(2)}) copy-start(f32[2,64,1024]{2,1,0:T(8,128)S(1)} %collective-permute-done.9.refs_8_.refs_9_) | copy-start | bytes 1572868
  26.3 11.7 %collective-permute-start.10 = (f32[2,64,1024]{2,1,0:T(8,128)S(1)}, f32[2,64,1024]{2,1,0:T(8,128)S(1)}, u32[]{:S(2)}, u32[]{:S(2)}) collective-permute-start(f32[2,64,1024]{2,1,0:T(8,128)S(1)} %collective-permute-done.9.refs_8_.refs_9_), channel_id=1, source_target_pairs={{0,2},{1,31},{2,4},{3,1},{4,6},{5,3},{6,8},{7,5},{8,10},{9,7},{10,... | collective-permute-start | bytes 1572872 | tf_op jit(solution)/shard_map/ppermute | solution.py:247
  32.4 43.5 %copy-start.3 = (f32[2,64,1024]{2,1,0:T(8,128)}, f32[2,64,1024]{2,1,0:T(8,128)S(1)}, u32[]{:S(2)}) copy-start(f32[2,64,1024]{2,1,0:T(8,128)S(1)} %collective-permute-done.2.refs_2_) | copy-start | bytes 1572868
  32.4 11.2 %collective-permute-start.3 = (f32[2,64,1024]{2,1,0:T(8,128)S(1)}, f32[2,64,1024]{2,1,0:T(8,128)S(1)}, u32[]{:S(2)}, u32[]{:S(2)}) collective-permute-start(f32[2,64,1024]{2,1,0:T(8,128)S(1)} %collective-permute-done.2.refs_2_), channel_id=1, source_target_pairs={{0,2},{1,31},{2,4},{3,1},{4,6},{5,3},{6,8},{7,5},{8,10},{9,7},{10,... | collective-permute-start | bytes 1572872 | tf_op jit(solution)/shard_map/ppermute | solution.py:245
  38.0 37.9 %copy-start.4 = (f32[2,64,1024]{2,1,0:T(8,128)}, f32[2,64,1024]{2,1,0:T(8,128)S(1)}, u32[]{:S(2)}) copy-start(f32[2,64,1024]{2,1,0:T(8,128)S(1)} %collective-permute-done.10.refs_9_.refs_10_) | copy-start | bytes 1572868
  38.0 11.2 %collective-permute-start.11 = (f32[2,64,1024]{2,1,0:T(8,128)S(1)}, f32[2,64,1024]{2,1,0:T(8,128)S(1)}, u32[]{:S(2)}, u32[]{:S(2)}) collective-permute-start(f32[2,64,1024]{2,1,0:T(8,128)S(1)} %collective-permute-done.10.refs_9_.refs_10_), channel_id=1, source_target_pairs={{0,2},{1,31},{2,4},{3,1},{4,6},{5,3},{6,8},{7,5},{8,10},{9,7},{10,... | collective-permute-start | bytes 1572872 | tf_op jit(solution)/shard_map/ppermute | solution.py:247
  43.6 32.2 %copy-start.5 = (f32[2,64,1024]{2,1,0:T(8,128)}, f32[2,64,1024]{2,1,0:T(8,128)S(1)}, u32[]{:S(2)}) copy-start(f32[2,64,1024]{2,1,0:T(8,128)S(1)} %collective-permute-done.3.refs_3_) | copy-start | bytes 1572868
  43.7 20.8 %collective-permute-start.4 = (f32[2,64,1024]{2,1,0:T(8,128)S(1)}, f32[2,64,1024]{2,1,0:T(8,128)}, u32[]{:S(2)}, u32[]{:S(2)}) collective-permute-start(f32[2,64,1024]{2,1,0:T(8,128)S(1)} %collective-permute-done.3.refs_3_), channel_id=1, source_target_pairs={{0,2},{1,31},{2,4},{3,1},{4,6},{5,3},{6,8},{7,5},{8,10},{9,7},{10,... | collective-permute-start | bytes 1572872 | tf_op jit(solution)/shard_map/ppermute | solution.py:245
  49.3 26.6 %copy-start.6 = (f32[2,64,1024]{2,1,0:T(8,128)}, f32[2,64,1024]{2,1,0:T(8,128)S(1)}, u32[]{:S(2)}) copy-start(f32[2,64,1024]{2,1,0:T(8,128)S(1)} %collective-permute-done.11.refs_10_.refs_11_) | copy-start | bytes 1572868
  49.3 17.1 %collective-permute-start.12 = (f32[2,64,1024]{2,1,0:T(8,128)S(1)}, f32[2,64,1024]{2,1,0:T(8,128)}, u32[]{:S(2)}, u32[]{:S(2)}) collective-permute-start(f32[2,64,1024]{2,1,0:T(8,128)S(1)} %collective-permute-done.11.refs_10_.refs_11_), channel_id=1, source_target_pairs={{0,2},{1,31},{2,4},{3,1},{4,6},{5,3},{6,8},{7,5},{8,10},{9,7},{10,... | collective-permute-start | bytes 1572872 | tf_op jit(solution)/shard_map/ppermute | solution.py:247
  54.3 14.8 %collective-permute-start.19 = (f32[2,64,1024]{2,1,0:T(8,128)}, f32[2,64,1024]{2,1,0:T(8,128)}, u32[]{:S(2)}, u32[]{:S(2)}) collective-permute-start(f32[2,64,1024]{2,1,0:T(8,128)} %bitcast.21), channel_id=1, source_target_pairs={{0,64},{1,257},{32,96},{33,289},{64,0},{65,321},{96,32},{97,353},{... | collective-permute-start | bytes 1572872 | tf_op jit(solution)/shard_map/ppermute | solution.py:248
  59.1 15.1 %collective-permute-start.20 = (f32[2,64,1024]{2,1,0:T(8,128)}, f32[2,64,1024]{2,1,0:T(8,128)}, u32[]{:S(2)}, u32[]{:S(2)}) collective-permute-start(f32[2,64,1024]{2,1,0:T(8,128)} %bitcast.22), channel_id=1, source_target_pairs={{0,96},{1,385},{32,0},{33,417},{64,32},{65,449},{96,64},{97,481},{... | collective-permute-start | bytes 1572872 | tf_op jit(solution)/shard_map/ppermute | solution.py:248
  61.8 12.4 %collective-permute-start.18 = (f32[2,64,1024]{2,1,0:T(8,128)}, f32[2,64,1024]{2,1,0:T(8,128)}, u32[]{:S(2)}, u32[]{:S(2)}) collective-permute-start(f32[2,64,1024]{2,1,0:T(8,128)} %bitcast.23), channel_id=1, source_target_pairs={{0,32},{1,129},{32,64},{33,161},{64,96},{65,193},{96,0},{97,225},{... | collective-permute-start | bytes 1572872 | tf_op jit(solution)/shard_map/ppermute | solution.py:248
  64.4 21.6 %collective-permute-start.5 = (f32[2,64,1024]{2,1,0:T(8,128)}, f32[2,64,1024]{2,1,0:T(8,128)}, u32[]{:S(2)}, u32[]{:S(2)}) collective-permute-start(f32[2,64,1024]{2,1,0:T(8,128)} %collective-permute-done.4.refs_4_), channel_id=1, source_target_pairs={{0,2},{1,31},{2,4},{3,1},{4,6},{5,3},{6,8},{7,5},{8,10},{9,7},{10,... | collective-permute-start | bytes 1572872 | tf_op jit(solution)/shard_map/ppermute | solution.py:245
  66.4 23.6 %collective-permute-start.13 = (f32[2,64,1024]{2,1,0:T(8,128)}, f32[2,64,1024]{2,1,0:T(8,128)}, u32[]{:S(2)}, u32[]{:S(2)}) collective-permute-start(f32[2,64,1024]{2,1,0:T(8,128)} %collective-permute-done.12.refs_11_.refs_12_), channel_id=1, source_target_pairs={{0,2},{1,31},{2,4},{3,1},{4,6},{5,3},{6,8},{7,5},{8,10},{9,7},{10,... | collective-permute-start | bytes 1572872 | tf_op jit(solution)/shard_map/ppermute | solution.py:247
  69.1 14.1 %collective-permute-start = (s32[37]{0:T(128)S(1)}, s32[37]{0:T(128)S(1)}, u32[]{:S(2)}, u32[]{:S(2)}) collective-permute-start(s32[37]{0:T(128)S(1)} %concatenate.3.info), channel_id=1, source_target_pairs={{0,1},{1,0},{2,3},{3,2},{4,5},{5,4},{6,7},{7,6},{8,9},{9,8},{10,11... | collective-permute-start | bytes 452 | tf_op jit(solution)/shard_map/ppermute | solution.py:250
  75.9 53.4 %copy-start = (f32[1,1,2,64,1024]{4,3,2,1,0:T(8,128)S(1)}, f32[1,1,2,64,1024]{4,3,2,1,0:T(8,128)}, u32[]{:S(2)}) copy-start(f32[1,1,2,64,1024]{4,3,2,1,0:T(8,128)} %param.11) | copy-start | bytes 1572868
  75.9 49.0 %collective-permute-start.21 = (f32[4,2,64,1024]{3,2,1,0:T(8,128)S(1)}, f32[4,2,64,1024]{3,2,1,0:T(8,128)S(1)}, u32[]{:S(2)}, u32[]{:S(2)}) collective-permute-start(f32[4,2,64,1024]{3,2,1,0:T(8,128)S(1)} %pad_maximum_fusion.u0), channel_id=1, source_target_pairs={{0,128},{1,33},{32,160},{33,65},{64,192},{65,97},{96,224},{97,1},{... | collective-permute-start | bytes 6291464 | tf_op jit(solution)/shard_map/ppermute | solution.py:249
  78.6 48.8 %collective-permute-start.22 = (f32[4,2,64,1024]{3,2,1,0:T(8,128)S(1)}, f32[4,2,64,1024]{3,2,1,0:T(8,128)S(1)}, u32[]{:S(2)}, u32[]{:S(2)}) collective-permute-start(f32[4,2,64,1024]{3,2,1,0:T(8,128)S(1)} %pad_maximum_fusion.u0), channel_id=1, source_target_pairs={{0,256},{1,65},{32,288},{33,97},{64,320},{65,1},{96,352},{97,33},{... | collective-permute-start | bytes 6291464 | tf_op jit(solution)/shard_map/ppermute | solution.py:249
  83.2 46.2 %collective-permute-start.23 = (f32[4,2,64,1024]{3,2,1,0:T(8,128)S(1)}, f32[4,2,64,1024]{3,2,1,0:T(8,128)S(1)}, u32[]{:S(2)}, u32[]{:S(2)}) collective-permute-start(f32[4,2,64,1024]{3,2,1,0:T(8,128)S(1)} %pad_maximum_fusion.u0), channel_id=1, source_target_pairs={{0,384},{1,97},{32,416},{33,1},{64,448},{65,33},{96,480},{97,65},{... | collective-permute-start | bytes 6291464 | tf_op jit(solution)/shard_map/ppermute | solution.py:249
  86.0 10.4 %collective-permute-start.6 = (f32[2,64,1024]{2,1,0:T(8,128)}, f32[2,64,1024]{2,1,0:T(8,128)S(1)}, u32[]{:S(2)}, u32[]{:S(2)}) collective-permute-start(f32[2,64,1024]{2,1,0:T(8,128)} %collective-permute-done.5.refs_5_), channel_id=1, source_target_pairs={{0,2},{1,31},{2,4},{3,1},{4,6},{5,3},{6,8},{7,5},{8,10},{9,7},{10,... | collective-permute-start | bytes 1572872 | tf_op jit(solution)/shard_map/ppermute | solution.py:245
  90.0 12.1 %collective-permute-start.14 = (f32[2,64,1024]{2,1,0:T(8,128)}, f32[2,64,1024]{2,1,0:T(8,128)S(1)}, u32[]{:S(2)}, u32[]{:S(2)}) collective-permute-start(f32[2,64,1024]{2,1,0:T(8,128)} %collective-permute-done.13.refs_12_.refs_13_), channel_id=1, source_target_pairs={{0,2},{1,31},{2,4},{3,1},{4,6},{5,3},{6,8},{7,5},{8,10},{9,7},{10,... | collective-permute-start | bytes 1572872 | tf_op jit(solution)/shard_map/ppermute | solution.py:247
  96.4 16.9 %copy-start.7 = (f32[2,64,1024]{2,1,0:T(8,128)}, f32[2,64,1024]{2,1,0:T(8,128)S(1)}, u32[]{:S(2)}) copy-start(f32[2,64,1024]{2,1,0:T(8,128)S(1)} %collective-permute-done.6.refs_6_) | copy-start | bytes 1572868
  96.4 11.2 %collective-permute-start.7 = (f32[2,64,1024]{2,1,0:T(8,128)S(1)}, f32[2,64,1024]{2,1,0:T(8,128)S(1)}, u32[]{:S(2)}, u32[]{:S(2)}) collective-permute-start(f32[2,64,1024]{2,1,0:T(8,128)S(1)} %collective-permute-done.6.refs_6_), channel_id=1, source_target_pairs={{0,2},{1,31},{2,4},{3,1},{4,6},{5,3},{6,8},{7,5},{8,10},{9,7},{10,... | collective-permute-start | bytes 1572872 | tf_op jit(solution)/shard_map/ppermute | solution.py:245
  102.1 11.3 %copy-start.8 = (f32[2,64,1024]{2,1,0:T(8,128)}, f32[2,64,1024]{2,1,0:T(8,128)S(1)}, u32[]{:S(2)}) copy-start(f32[2,64,1024]{2,1,0:T(8,128)S(1)} %collective-permute-done.14.refs_13_.refs_14_) | copy-start | bytes 1572868
  102.1 11.2 %collective-permute-start.15 = (f32[2,64,1024]{2,1,0:T(8,128)S(1)}, f32[2,64,1024]{2,1,0:T(8,128)S(1)}, u32[]{:S(2)}, u32[]{:S(2)}) collective-permute-start(f32[2,64,1024]{2,1,0:T(8,128)S(1)} %collective-permute-done.14.refs_13_.refs_14_), channel_id=1, source_target_pairs={{0,2},{1,31},{2,4},{3,1},{4,6},{5,3},{6,8},{7,5},{8,10},{9,7},{10,... | collective-permute-start | bytes 1572872 | tf_op jit(solution)/shard_map/ppermute | solution.py:247
  115.2 38.5 %collective-permute-start.16 = (f32[4,2,64,1024]{3,2,1,0:T(8,128)S(1)}, f32[4,2,64,1024]{3,2,1,0:T(8,128)S(1)}, u32[]{:S(2)}, u32[]{:S(2)}) collective-permute-start(f32[4,2,64,1024]{3,2,1,0:T(8,128)S(1)} %shard_map.77), channel_id=1, source_target_pairs={{0,1},{1,0},{2,3},{3,2},{4,5},{5,4},{6,7},{7,6},{8,9},{9,8},{10,11... | collective-permute-start | bytes 6291464 | tf_op jit(solution)/shard_map/ppermute | solution.py:269
  131.3 20.5 %collective-permute-start.24 = (f32[2,2,64,1024]{3,2,1,0:T(8,128)S(1)}, f32[2,2,64,1024]{3,2,1,0:T(8,128)S(1)}, u32[]{:S(2)}, u32[]{:S(2)}) collective-permute-start(f32[2,2,64,1024]{3,2,1,0:T(8,128)S(1)} %get-tuple-element.14), channel_id=1, source_target_pairs={{0,1},{1,0},{2,3},{3,2},{4,5},{5,4},{6,7},{7,6},{8,9},{9,8},{10,11... | collective-permute-start | bytes 3145736 | tf_op jit(solution)/shard_map/ppermute | solution.py:267
  137.6 11.0 %collective-permute-start.8 = (f32[2,64,1024]{2,1,0:T(8,128)S(1)}, f32[2,64,1024]{2,1,0:T(8,128)S(1)}, u32[]{:S(2)}, u32[]{:S(2)}) collective-permute-start(f32[2,64,1024]{2,1,0:T(8,128)S(1)} %collective-permute-done.7.refs_7_), channel_id=1, source_target_pairs={{0,2},{1,31},{2,4},{3,1},{4,6},{5,3},{6,8},{7,5},{8,10},{9,7},{10,... | collective-permute-start | bytes 1572872 | tf_op jit(solution)/shard_map/ppermute | solution.py:245
  148.6 5.0 %collective-permute-start.17 = (f32[2,64,1024]{2,1,0:T(8,128)S(1)}, f32[2,64,1024]{2,1,0:T(8,128)S(1)}, u32[]{:S(2)}, u32[]{:S(2)}) collective-permute-start(f32[2,64,1024]{2,1,0:T(8,128)S(1)} %collective-permute-done.8.refs_8_), channel_id=1, source_target_pairs={{0,1},{1,0},{2,3},{3,2},{4,5},{5,4},{6,7},{7,6},{8,9},{9,8},{10,11... | collective-permute-start | bytes 1572872 | tf_op jit(solution)/shard_map/ppermute | solution.py:270
